TPU v7x, 32 devices: a whole 2x2x4 slice. The times are simulated.
32 devices in a mesh: seq: 16 (over z, x, core), ch: 2 (over y).
Axes of the slice: x: 2, y: 2, z: 4, core: 2. Of those that a mesh axis runs over, the one named last changes fastest.
Arguments:
- queries: bfloat16 [4096, 4096], P('seq', 'ch'), may hold values from -6 to 6
- key_in: bfloat16 [4096, 4096], P('seq', 'ch'), may hold values from -6 to 6
- value_in: bfloat16 [4096, 4096], P('seq', 'ch'), may hold values from -6 to 6
- filter_raw: bfloat16 [4096, 4096], P('seq', 'ch'), may hold values from -6 to 6
- skip_gain: float32 [4096], P('ch'), may hold values from -4 to 4
- out_weight: bfloat16 [4096, 4096], P('ch'), may hold values from -0.09375 to 0.09375
- cotangent: bfloat16 [4096, 4096], P('seq', 'ch'), may hold values from -6 to 6
Outputs:
- projected: bfloat16 [4096, 4096], P('seq', 'ch')
- grad_query: bfloat16 [4096, 4096], P('seq', 'ch')
- grad_key: bfloat16 [4096, 4096], P('seq', 'ch')
- grad_value: bfloat16 [4096, 4096], P('seq', 'ch')
- grad_filter: bfloat16 [4096, 4096], P('seq', 'ch')
All inputs are finite; a program needn't handle non-finite values.
Results may differ from a plain program's by a relative error of at most 0.015.
Values may be sent and summed in bfloat16 or wider, within the bound.
A program may use at most 192 MiB of HBM per device.

v0:
```python
import math

import jax
import jax.numpy as jnp
from jax import lax
from jax.sharding import PartitionSpec as P

precise = lax.Precision.HIGHEST


def phase_table(height, breadth, period, row_start, column_start):
    row_index = (row_start + lax.iota(jnp.int32, height))[:, None]
    column_index = (column_start + lax.iota(jnp.int32, breadth))[None, :]
    residue = row_index * column_index % period
    angles = residue.astype(jnp.float32) * (2.0 * math.pi / period)
    return (jnp.cos(angles), jnp.sin(angles))


def over_blocks(pieces, total_blocks):
    cosine_table, sine_table = phase_table(total_blocks, pieces.shape[1], total_blocks, 0, 0)
    values = pieces.astype(jnp.float32)
    real_part = jnp.einsum("kj,sj...->sk...", cosine_table, values, precision=precise)
    imag_part = -jnp.einsum("kj,sj...->sk...", sine_table, values, precision=precise)
    return (real_part, imag_part)


def under_blocks(real_part, imag_part, kept_blocks):
    cosine_table, sine_table = phase_table(
        kept_blocks, real_part.shape[1], real_part.shape[1], 0, 0
    )
    first_term = jnp.einsum("jk,sk...->sj...", cosine_table, real_part, precision=precise)
    second_term = jnp.einsum("jk,sk...->sj...", sine_table, imag_part, precision=precise)
    return first_term - second_term


def rotate(real_part, imag_part, freq_start, row_start, period, direction):
    row_count = real_part.shape[3]
    cosine_table, sine_table = phase_table(
        real_part.shape[1], row_count, period, freq_start, row_start
    )
    cosine_table = cosine_table[None, :, None, :]
    sine_table = direction * sine_table[None, :, None, :]
    return (
        real_part * cosine_table - imag_part * sine_table,
        real_part * sine_table + imag_part * cosine_table,
    )


def over_rows(real_part, imag_part, direction):
    length_rows = real_part.shape[3]
    cosine_table, sine_table = phase_table(length_rows, length_rows, length_rows, 0, 0)
    sine_table = direction * sine_table
    form = "mr,skcr->skcm"

    def contract(table, values):
        return jnp.einsum(form, table, values, precision=precise)

    new_real = contract(cosine_table, real_part) - contract(sine_table, imag_part)
    new_imag = contract(cosine_table, imag_part) + contract(sine_table, real_part)
    return (new_real, new_imag)


def transform(signals):
    seq_devices = lax.axis_size("seq")
    local_rows = signals.shape[1]
    total_blocks = 2 * seq_devices
    period = total_blocks * local_rows
    flipped = jnp.transpose(signals, (0, 2, 1))[:, None]
    pieces = lax.all_to_all(flipped, "seq", split_axis=2, concat_axis=1, tiled=True)
    real_part, imag_part = over_blocks(pieces, total_blocks)
    real_part, imag_part = rotate(real_part, imag_part, 0, 0, period, -1.0)
    return over_rows(real_part, imag_part, -1.0)


def inverse(real_part, imag_part):
    seq_devices = lax.axis_size("seq")
    local_rows = real_part.shape[3]
    period = 2 * seq_devices * local_rows
    real_part, imag_part = over_rows(real_part, imag_part, 1.0)
    real_part, imag_part = rotate(real_part, imag_part, 0, 0, period, 1.0)
    values = under_blocks(real_part, imag_part, seq_devices)
    values = lax.all_to_all(values, "seq", split_axis=1, concat_axis=2, tiled=True)
    return jnp.transpose(values[:, 0], (0, 2, 1))


def on_device(queries, key_in, value_in, filter_raw, skip_gain, out_weight, cotangent):
    local_rows, local_width = queries.shape
    seq_devices = lax.axis_size("seq")
    full_length = local_rows * seq_devices
    factor = 1.0 / (math.sqrt(full_length) * 2.0 * full_length)
    grad_mixed = lax.dot_general(
        lax.all_gather(cotangent, "ch", axis=1, tiled=True),
        out_weight,
        (((1,), (1,)), ((), ())),
        preferred_element_type=jnp.float32,
    )
    product_kv = (key_in.astype(jnp.float32) * value_in.astype(jnp.float32)).astype(jnp.bfloat16)
    grad_conv = (grad_mixed * queries.astype(jnp.float32)).astype(jnp.bfloat16)
    real_part, imag_part = transform(jnp.stack([product_kv, filter_raw, grad_conv]))
    z_real, h_real, g_real = (real_part[0], real_part[1], real_part[2])
    z_imag, h_imag, g_imag = (imag_part[0], imag_part[1], imag_part[2])
    conv_real = h_real * z_real - h_imag * z_imag
    conv_imag = h_real * z_imag + h_imag * z_real
    back_real = h_real * g_real + h_imag * g_imag
    back_imag = h_real * g_imag - h_imag * g_real
    taps_real = z_real * g_real + z_imag * g_imag
    taps_imag = z_real * g_imag - z_imag * g_real
    results = inverse(
        jnp.stack([conv_real, back_real, taps_real]), jnp.stack([conv_imag, back_imag, taps_imag])
    )
    results = results * factor
    convolved = results[0] + skip_gain * product_kv.astype(jnp.float32)
    gated_output = (queries.astype(jnp.float32) * convolved).astype(jnp.bfloat16)
    partial_terms = jnp.dot(gated_output, out_weight, preferred_element_type=jnp.float32)
    projected = lax.psum_scatter(partial_terms, "ch", scatter_dimension=1, tiled=True).astype(
        jnp.bfloat16
    )
    grad_query = (grad_mixed * convolved).astype(jnp.bfloat16)
    grad_product = results[1] + skip_gain * grad_conv.astype(jnp.float32)
    grad_key = (grad_product * value_in.astype(jnp.float32)).astype(jnp.bfloat16)
    grad_value = (grad_product * key_in.astype(jnp.float32)).astype(jnp.bfloat16)
    grad_filter = results[2].astype(jnp.bfloat16)
    return (projected, grad_query, grad_key, grad_value, grad_filter)


def solution(mesh):
    placed = (
        P("seq", "ch"),
        P("seq", "ch"),
        P("seq", "ch"),
        P("seq", "ch"),
        P("ch"),
        P("ch", None),
        P("seq", "ch"),
    )
    return jax.shard_map(
        on_device,
        mesh=mesh,
        in_specs=placed,
        out_specs=(P("seq", "ch"), P("seq", "ch"), P("seq", "ch"), P("seq", "ch"), P("seq", "ch")),
        check_vma=False,
    )
```

profile of v0, /device:TPU:0, one launch (start us, length us, event | category | flops | bytes accessed | tf_op | source)
XLA Modules:
  0.0 686.0 jit_solution(9719354714122035270)
XLA Ops:
  7.2 0.0 all-gather.2.cloned.1.call-start
  7.2 0.7 all-gather.2.cloned.1.call-update
  7.9 2.9 fusion.168
  10.8 34.6 %all-gather.2.cloned.1.call-done = bf16[256,4096]{1,0:T(8,128)(2,1)} async-done(((bf16[256,2048]{1,0:T(8,128)(2,1)}), bf16[256,4096]{1,0:T(8,128)(2,1)}) %all-gather.2.cloned.1.call-update) | async-done | bytes 2097168 | tf_op jit(solution)/shard_map/all_gather | solution.py:92
  45.4 12.8 %fusion.46 = (bf16[256,2048]{1,0:T(8,128)(2,1)}, f32[256,2048]{1,0:T(8,128)}) fusion(bf16[256,2048]{1,0:T(8,128)(2,1)} %param.7, bf16[256,4096]{1,0:T(8,128)(2,1)} %all-gather.2.cloned.1.call-done, bf16[2048,4096]{1,0:T(8,128)(2,1)} %param.12), kind=kOutput, calls=%fused_computation.60 | convolution fusion | flops 4296540160 | bytes 23068672 | tf_op jit(solution)/shard_map/dot_general | solution.py:91
  58.1 2.2 maximum_bitcast_fusion
  60.3 4.8 copy.34
  65.2 5.7 all-to-all-start
  70.9 0.2 reduce-scatter.2.cloned.1.call-start
  71.1 0.1 fusion.91
  71.2 0.1 broadcast_multiply_fusion.1
  71.4 77.0 %all-to-all-done = bf16[3,1,2048,256]{3,0,1,2:T(4,128)(2,1)} async-done(((bf16[3,1,2048,256]{3,0,1,2:T(4,128)(2,1)}), bf16[3,1,2048,256]{3,0,1,2:T(4,128)(2,1)}, u32[]{:S(2)}, u32[]{:S(2)}) %all-to-all-start) | async-done | bytes 3145760 | tf_op jit(solution)/shard_map/all_to_all | solution.py:69
  148.4 2.6 copy.35
  151.0 0.0 copy-start.2
  151.0 8.4 %fusion.40 = f32[3,128,256,32]{2,3,1,0:T(8,128)} fusion(bf16[3,16,128,256]{3,2,1,0:T(8,128)(2,1)S(1)} %bitcast.101), kind=kOutput, calls=%fused_computation.51 | convolution fusion | flops 603986944 | bytes 15728640 | tf_op jit(solution)/shard_map/kj,sj...->sk.../dot_general | solution.py:23
  159.4 0.0 copy-done.2
  159.4 14.6 %fusion = (f32[3,32,128,256]{3,1,2,0:T(8,128)}, f32[3,32,128,256]{3,1,2,0:T(8,128)S(1)}) fusion(f32[3,128,256,32]{2,3,1,0:T(8,128)} %fusion.40, f32[32,256]{1,0:T(8,128)S(1)} %get-tuple-element.18, f32[32,256]{1,0:T(8,128)S(1)} %get-tuple-element.19, bf16[3,16,128,256]{3,2,1,0:T(8,128)(2,1)} %bitcast.102), kind=kOutput, calls=%fused_computation.4 | convolution fusion | flops 626007040 | bytes 40960000 | tf_op jit(solution)/shard_map/kj,sj...->sk.../dot_general | solution.py:22
  174.0 19.4 %fusion.20 = f32[3,32,128,256]{3,2,1,0:T(8,128)} fusion(f32[3,32,128,256]{3,1,2,0:T(8,128)S(1)} %get-tuple-element.6), kind=kOutput, calls=%fused_computation.26 | convolution fusion | flops 9664659456 | bytes 25165824 | tf_op jit(solution)/shard_map/mr,skcr->skcm/dot_general | solution.py:56
  193.5 19.0 %fusion.18 = f32[3,32,128,256]{3,2,1,0:T(8,128)} fusion(f32[3,32,128,256]{3,1,2,0:T(8,128)S(1)} %get-tuple-element.6), kind=kOutput, calls=%fused_computation.24 | convolution fusion | flops 9664593920 | bytes 25165824 | tf_op jit(solution)/shard_map/mr,skcr->skcm/dot_general | solution.py:56
  212.5 24.3 %fusion.34 = f32[3,32,128,256]{3,2,1,0:T(8,128)S(1)} fusion(f32[3,32,128,256]{3,2,1,0:T(8,128)} %fusion.20, f32[3,32,128,256]{3,1,2,0:T(8,128)} %get-tuple-element.5), kind=kOutput, calls=%fused_computation.47 | convolution fusion | flops 9667739648 | bytes 37748736 | tf_op jit(solution)/shard_map/mr,skcr->skcm/dot_general | solution.py:56
  236.8 26.1 %fusion.37 = f32[3,32,128,256]{3,2,1,0:T(8,128)} fusion(f32[3,32,128,256]{3,2,1,0:T(8,128)} %fusion.18, f32[3,32,128,256]{3,1,2,0:T(8,128)} %get-tuple-element.5), kind=kOutput, calls=%fused_computation.48 | convolution fusion | flops 9667805184 | bytes 37748736 | tf_op jit(solution)/shard_map/mr,skcr->skcm/dot_general | solution.py:56
  262.9 10.4 %multiply_subtract_fusion.2 = (f32[1,32,128,256]{3,2,1,0:T(8,128)}, f32[1,32,128,256]{3,2,1,0:T(8,128)}, f32[1,32,128,256]{3,2,1,0:T(8,128)}, f32[1,32,128,256]{3,2,1,0:T(8,128)}) fusion(f32[3,32,128,256]{3,2,1,0:T(8,128)} %fusion.37, f32[3,32,128,256]{3,2,1,0:T(8,128)S(1)} %fusion.34), kind=kLoop, calls=%fused_computation.46 | loop fusion | flops 12582912 | bytes 41943040 | tf_op jit(solution)/shard_map/sub | solution.py:102
  273.3 8.1 %multiply_add_fusion.2 = (f32[1,32,128,256]{3,2,1,0:T(8,128)}, f32[1,32,128,256]{3,2,1,0:T(8,128)}) fusion(f32[3,32,128,256]{3,2,1,0:T(8,128)} %fusion.37, f32[3,32,128,256]{3,2,1,0:T(8,128)S(1)} %fusion.34), kind=kLoop, calls=%fused_computation.45 | loop fusion | flops 6291456 | bytes 33554432 | tf_op jit(solution)/shard_map/add | solution.py:104
  281.4 10.8 %pad_maximum_fusion = f32[3,32,128,256]{3,2,1,0:T(8,128)} fusion(f32[1,32,128,256]{3,2,1,0:T(8,128)} %get-tuple-element.8, f32[1,32,128,256]{3,2,1,0:T(8,128)} %get-tuple-element.11, f32[1,32,128,256]{3,2,1,0:T(8,128)} %get-tuple-element.7), kind=kLoop, calls=%fused_computation | loop fusion | flops 6291456 | bytes 25165824 | tf_op jit(solution)/shard_map/stack | solution.py:109
  292.2 0.0 copy-start
  292.2 25.6 %fusion.14 = f32[3,32,128,256]{3,1,2,0:T(8,128)} fusion(f32[3,32,128,256]{3,2,1,0:T(8,128)} %pad_maximum_fusion), kind=kOutput, calls=%fused_computation.20 | convolution fusion | flops 9664593920 | bytes 25165824 | tf_op jit(solution)/shard_map/mr,skcr->skcm/dot_general | solution.py:56
  317.8 0.0 copy-done
  317.8 0.0 copy-start.3
  317.8 19.2 %fusion.16 = f32[3,32,128,256]{3,1,2,0:T(8,128)} fusion(f32[3,32,128,256]{3,2,1,0:T(8,128)S(1)} %copy-done), kind=kOutput, calls=%fused_computation.22 | convolution fusion | flops 9664593920 | bytes 25165824 | tf_op jit(solution)/shard_map/mr,skcr->skcm/dot_general | solution.py:56
  337.0 0.0 copy-done.3
  337.0 9.5 %pad_maximum_fusion.1 = f32[3,32,128,256]{3,2,1,0:T(8,128)} fusion(f32[1,32,128,256]{3,2,1,0:T(8,128)} %get-tuple-element.10, f32[1,32,128,256]{3,2,1,0:T(8,128)S(1)} %copy-done.3, f32[1,32,128,256]{3,2,1,0:T(8,128)} %get-tuple-element.12), kind=kLoop, calls=%fused_computation.1 | loop fusion | flops 6291456 | bytes 25165824 | tf_op jit(solution)/shard_map/stack | solution.py:109
  346.5 0.0 copy-start.1
  346.5 0.0 slice-start
  346.5 0.0 slice-start.1
  346.5 25.9 %fusion.10 = f32[3,32,128,256]{3,1,2,0:T(8,128)} fusion(f32[3,32,128,256]{3,2,1,0:T(8,128)} %pad_maximum_fusion.1), kind=kOutput, calls=%fused_computation.16 | convolution fusion | flops 9664593920 | bytes 25165824 | tf_op jit(solution)/shard_map/mr,skcr->skcm/dot_general | solution.py:56
  372.4 0.0 copy-done.1
  372.4 0.0 slice-start.2
  372.4 19.1 %fusion.12 = f32[3,32,128,256]{3,1,2,0:T(8,128)} fusion(f32[3,32,128,256]{3,2,1,0:T(8,128)S(1)} %copy-done.1), kind=kOutput, calls=%fused_computation.18 | convolution fusion | flops 9664593920 | bytes 25165824 | tf_op jit(solution)/shard_map/mr,skcr->skcm/dot_general | solution.py:56
  391.6 0.0 slice-done
  391.6 0.0 slice-done.1
  391.6 0.0 slice-done.2
  391.6 18.2 %fusion.2 = f32[3,128,256,16]{2,3,1,0:T(8,128)} fusion(f32[32,256]{1,0:T(8,128)S(1)} %fusion.91, f32[32,256]{1,0:T(8,128)S(1)} %get-tuple-element.19, f32[3,32,128,256]{3,1,2,0:T(8,128)} %fusion.10, f32[3,32,128,256]{3,1,2,0:T(8,128)S(1)} %bitcast.100, f32[3,32,128,256]{3,1,2,0:T(8,128)} %fusion.16, f32[3,32,128,256]{3,1,2,0:T(8,128)} %fusion.12), kind=kOutput, calls=%fused_computation.8 | convolution fusion | flops 619715584 | bytes 56688640 | tf_op jit(solution)/shard_map/jk,sk...->sj.../dot_general | solution.py:32
  409.8 20.7 %subtract_bitcast_fusion = f32[3,16,128,256]{3,1,2,0:T(8,128)S(1)} fusion(f32[3,128,256,16]{2,3,1,0:T(8,128)} %fusion.2, f32[32,256]{1,0:T(8,128)S(1)} %fusion.91, f32[32,256]{1,0:T(8,128)S(1)} %get-tuple-element.19, f32[3,32,128,256]{3,1,2,0:T(8,128)} %fusion.10, f32[3,32,128,256]{3,1,2,0:T(8,128)} %fusion.14, f32[3,32,128,256]{3,1,2,0:T(8,128)} %fusion.16, ...), kind=kOutput, calls=%fused_computation.32 | convolution fusion | flops 621288448 | bytes 62980096 | tf_op jit(solution)/shard_map/jk,sk...->sj.../dot_general | solution.py:31
  430.5 3.6 copy.46
  434.1 156.7 %all_to_all.21 = f32[3,16,128,256]{3,2,0,1:T(8,128)S(1)} all-to-all(f32[3,16,128,256]{3,2,0,1:T(8,128)S(1)} %copy.46), channel_id=1, replica_groups=mesh['seq'=16,'ch'=2] {'seq'}, dimensions={1} | all-to-all | bytes 12582912 | tf_op jit(solution)/shard_map/all_to_all | solution.py:82
  590.9 3.4 broadcast_multiply_fusion
  594.3 0.0 copy-start.4
  594.3 0.0 copy-start.5
  594.3 0.0 copy-start.7
  594.3 6.8 copy.47
  601.1 7.1 %mul.460 = f32[3,2048,256]{1,2,0:T(8,128)} reshape(f32[3,16,128,256]{2,1,3,0:T(8,128)} %copy.47) | data formatting | bytes 12582912 | tf_op jit(solution)/shard_map/mul | solution.py:111
  608.2 0.0 copy-done.4
  608.2 0.0 copy-done.5
  608.2 0.0 copy-done.7
  608.2 0.0 copy-start.6
  608.2 13.4 %fusion.54 = f32[256,4096]{1,0:T(8,128)} fusion(bf16[2048,4096]{1,0:T(8,128)(2,1)} %param.12, bf16[256,2048]{1,0:T(8,128)(2,1)} %param.7, f32[3,256,2048]{2,1,0:T(8,128)} %bitcast.103, f32[2048]{0:T(1024)S(1)} %copy-done.7, bf16[256,2048]{1,0:T(8,128)(2,1)S(1)} %copy-done.4, bf16[256,2048]{1,0:T(8,128)(2,1)S(1)} %copy-done.5), kind=kOutput, calls=%fused_computation.72 | convolution fusion | flops 4300210176 | bytes 26222592 | tf_op jit(solution)/shard_map/dot_general | solution.py:114
  621.6 0.0 reduce-scatter.2.cloned.1.call-update
  621.7 2.7 fusion.53
  624.4 0.0 copy-done.6
  624.4 5.5 fusion.48
  629.9 46.3 %reduce-scatter.2.cloned.1.call-done = f32[256,2048]{1,0:T(8,128)} async-done(((f32[256,4096]{1,0:T(8,128)}), f32[256,2048]{1,0:T(8,128)}) %reduce-scatter.2.cloned.1.call-update) | async-done | bytes 2097168 | tf_op jit(solution)/shard_map/reduce_scatter | solution.py:115
  676.1 2.7 convert_element_type.111
  (1 shorter events, 0.0 us)
Async XLA Ops:
  7.2 38.2 %all-gather.2.cloned.1.call-start = ((), (), s32[]{:S(2)}) async-start(), calls=%async_computation.3 | async-start | bytes 3145728 | tf_op jit(solution)/shard_map/all_gather | solution.py:92
  65.2 83.2 %all-to-all-start = ((bf16[3,1,2048,256]{3,0,1,2:T(4,128)(2,1)}), bf16[3,1,2048,256]{3,0,1,2:T(4,128)(2,1)}, u32[]{:S(2)}, u32[]{:S(2)}) async-start(bf16[3,1,2048,256]{3,0,1,2:T(4,128)(2,1)} %copy.34), calls=%async_computation | async-start | bytes 8388608 | tf_op jit(solution)/shard_map/all_to_all | solution.py:69
  70.9 605.3 %reduce-scatter.2.cloned.1.call-start = ((), (), s32[]{:S(2)}) async-start(), calls=%async_computation.4 | async-start | bytes 6291456 | tf_op jit(solution)/shard_map/reduce_scatter | solution.py:115
  151.0 8.4 %copy-start.2 = (bf16[3,1,2048,256]{3,2,0,1:T(8,128)(2,1)}, bf16[3,1,2048,256]{3,2,0,1:T(8,128)(2,1)S(1)}, u32[]{:S(2)}) copy-start(bf16[3,1,2048,256]{3,2,0,1:T(8,128)(2,1)S(1)} %copy.35) | copy-start | bytes 9437188
  292.2 25.6 %copy-start = (f32[3,32,128,256]{3,2,1,0:T(8,128)S(1)}, f32[3,32,128,256]{3,2,1,0:T(8,128)}, u32[]{:S(2)}) copy-start(f32[3,32,128,256]{3,2,1,0:T(8,128)} %pad_maximum_fusion) | copy-start | bytes 37748740
  317.8 19.2 %copy-start.3 = (f32[1,32,128,256]{3,2,1,0:T(8,128)S(1)}, f32[1,32,128,256]{3,2,1,0:T(8,128)}, u32[]{:S(2)}) copy-start(f32[1,32,128,256]{3,2,1,0:T(8,128)} %get-tuple-element.9) | copy-start | bytes 12582916
  346.5 25.9 %copy-start.1 = (f32[3,32,128,256]{3,2,1,0:T(8,128)S(1)}, f32[3,32,128,256]{3,2,1,0:T(8,128)}, u32[]{:S(2)}) copy-start(f32[3,32,128,256]{3,2,1,0:T(8,128)} %pad_maximum_fusion.1) | copy-start | bytes 37748740
  346.5 45.1 %slice-start = ((s8[12582912]{0:T(1024)(128)(4,1)}), s8[4194304]{0:T(1024)(128)(4,1)S(1)}, s32[]{:S(2)}) async-start(s8[12582912]{0:T(1024)(128)(4,1)} %bitcast.99), calls=%async_computation.5 | async-start | bytes 8388608
  346.5 45.1 %slice-start.1 = ((s8[12582912]{0:T(1024)(128)(4,1)}), s8[4194304]{0:T(1024)(128)(4,1)S(1)}, s32[]{:S(2)}) async-start(s8[12582912]{0:T(1024)(128)(4,1)} %bitcast.99), calls=%async_computation.6 | async-start | bytes 8388608
  372.4 19.1 %slice-start.2 = ((s8[12582912]{0:T(1024)(128)(4,1)}), s8[4194304]{0:T(1024)(128)(4,1)S(1)}, s32[]{:S(2)}) async-start(s8[12582912]{0:T(1024)(128)(4,1)} %bitcast.99), calls=%async_computation.7 | async-start | bytes 8388608
  594.3 13.9 %copy-start.4 = (bf16[256,2048]{1,0:T(8,128)(2,1)S(1)}, bf16[256,2048]{1,0:T(8,128)(2,1)}, u32[]{:S(2)}) copy-start(bf16[256,2048]{1,0:T(8,128)(2,1)} %param.9) | copy-start | bytes 3145732
  594.3 13.9 %copy-start.5 = (bf16[256,2048]{1,0:T(8,128)(2,1)S(1)}, bf16[256,2048]{1,0:T(8,128)(2,1)}, u32[]{:S(2)}) copy-start(bf16[256,2048]{1,0:T(8,128)(2,1)} %param.8) | copy-start | bytes 3145732
  594.3 13.9 %copy-start.7 = (f32[2048]{0:T(1024)S(1)}, f32[2048]{0:T(1024)}, u32[]{:S(2)}) copy-start(f32[2048]{0:T(1024)} %param.11) | copy-start | bytes 24580
  608.2 16.2 %copy-start.6 = (bf16[256,2048]{1,0:T(8,128)(2,1)S(1)}, bf16[256,2048]{1,0:T(8,128)(2,1)}, u32[]{:S(2)}) copy-start(bf16[256,2048]{1,0:T(8,128)(2,1)} %get-tuple-element.16) | copy-start | bytes 3145732
Sparse Core Ops, SparseCore 0:
  9.5 35.8 all-gather.1
  621.8 54.3 reduce-scatter.1
where the time goes:
time: 691 us; the launch traced here: 686 us
  matrix products  267 us (39%)
  waiting for transfers between devices  159 us (23%)
  blocking collectives  157 us (23%)
  other arithmetic  55.8 us (8%)
  local copies, waits for them, and re-layouts  27.8 us (4%)
  between operations  14.4 us (2%)
    dot_general x8, matrix products, contract(): return jnp.einsum(form, table, values, precision=precise)  179 us
    all_to_all x1, blocking collectives, inverse(): lax.all_to_all(values, 'seq', split_axis=1, concat_axis=2, tiled=True)  157 us
    all_to_all x1, waiting for transfers between devices, transform(): lax.all_to_all(flipped, 'seq', split_axis=2, concat_axis=1, tiled=True)  77 us
    reduce_scatter x1, waiting for transfers between devices, on_device(): lax.psum_scatter(partial_terms, 'ch', scatter_dimension=1, tiled=True)  46.3 us
    all_gather x1, waiting for transfers between devices, on_device(): lax.all_gather(cotangent, 'ch', axis=1, tiled=True)  34.6 us
    dot_general x1, matrix products, under_blocks(): jnp.einsum('jk,sk...->sj...', cosine_table, real_part, precision=precise)  20.7 us
    dot_general x1, matrix products, under_blocks(): jnp.einsum('jk,sk...->sj...', sine_table, imag_part, precision=precise)  18.2 us
    dot_general x1, matrix products, over_blocks(): jnp.einsum('kj,sj...->sk...', cosine_table, values, precision=precise)  14.6 us
  transfers between devices with their start and end apart: 3, of which 3 were waited for; matrix products, arithmetic and copies ran while one was open for 2% of the time, Pallas kernels for 0%

commit v1 on v0

v1 whole, which is shorter than its diff:
```python
import math

import jax
import jax.numpy as jnp
import numpy as np
from jax import lax
from jax.sharding import PartitionSpec as P

bf16 = jnp.bfloat16
f32 = jnp.float32


def split_period(period):
    second = 1 << ((period.bit_length() - 1) // 2)
    return period // second, second


def outer_table(first):
    f1 = np.arange(first // 2 + 1)[:, None]
    a = np.arange(first // 2)[None, :]
    angles = (f1 * a % first) * (2.0 * math.pi / first)
    return np.stack([np.cos(angles), -np.sin(angles)])


def inner_table(first, second):
    period = first * second
    f1 = np.arange(first // 2 + 1)[:, None, None]
    f2 = np.arange(second)[None, :, None]
    b = np.arange(second)[None, None, :]
    angles = (b * (f1 + first * f2) % period) * (2.0 * math.pi / period)
    cosine, sine = np.cos(angles), np.sin(angles)
    top = np.stack([cosine, sine], axis=2)
    bottom = np.stack([-sine, cosine], axis=2)
    return np.stack([top, bottom], axis=1)


def forward(signal, outer, inner):
    count, length, width = signal.shape
    pieces = signal.reshape(count, outer.shape[2], inner.shape[4], width)
    mid = jnp.einsum("pfa,sabc->fpbsc", outer, pieces, preferred_element_type=f32)
    mid = mid.astype(bf16)
    return jnp.einsum("fqgpb,fpbsc->fqgsc", inner, mid, preferred_element_type=f32)


def inverse(spectra, outer, inner):
    count, width = spectra.shape[3:]
    mid = jnp.einsum("fqgpb,fqgsc->fpbsc", inner, spectra, preferred_element_type=f32)
    mid = mid.astype(bf16)
    out = jnp.einsum("pfa,fpbsc->sabc", outer, mid, preferred_element_type=f32)
    return out.reshape(count, -1, width)


def to_channels(signals):
    devices = lax.axis_size("seq")
    count, rows, width = signals.shape
    parts = signals.reshape(count, rows, devices, width // devices).transpose(2, 0, 1, 3)
    parts = lax.all_to_all(parts, "seq", split_axis=0, concat_axis=0, tiled=True)
    return parts.transpose(1, 0, 2, 3).reshape(count, devices * rows, width // devices)


def to_positions(signals):
    devices = lax.axis_size("seq")
    count, length, width = signals.shape
    parts = signals.reshape(count, devices, length // devices, width).transpose(1, 0, 2, 3)
    parts = lax.all_to_all(parts, "seq", split_axis=0, concat_axis=0, tiled=True)
    return parts.transpose(1, 2, 0, 3).reshape(count, length // devices, devices * width)


def shifted(value, shift):
    size = lax.axis_size("ch")
    return lax.ppermute(value, "ch", [(i, (i + shift) % size) for i in range(size)])


def gather_columns(value):
    size, me = lax.axis_size("ch"), lax.axis_index("ch")
    rows, width = value.shape
    full = jnp.zeros((rows, size * width), value.dtype)
    for shift in range(size):
        part = shifted(value, shift) if shift else value
        owner = (me - shift + size) % size
        full = lax.dynamic_update_slice(full, part, (0, owner * width))
    return full


def scatter_columns(value):
    size, me = lax.axis_size("ch"), lax.axis_index("ch")
    rows, width = value.shape[0], value.shape[1] // size
    total = lax.dynamic_slice(value, (0, me * width), (rows, width))
    for shift in range(1, size):
        target = (me + shift) % size
        part = lax.dynamic_slice(value, (0, target * width), (rows, width)).astype(bf16)
        total = total + shifted(part, shift).astype(f32)
    return total


def on_device(queries, key_in, value_in, filter_raw, skip_gain, out_weight, cotangent):
    local_rows, local_width = queries.shape
    seq_devices = lax.axis_size("seq")
    length = local_rows * seq_devices
    group = local_width // seq_devices
    first, second = split_period(2 * length)
    table = outer_table(first)
    weight = np.full((first // 2 + 1, 1), 2.0)
    weight[0] = weight[-1] = 1.0
    outer = jnp.asarray(table, bf16)
    outer_back = jnp.asarray(table * weight, bf16)
    inner = jnp.asarray(inner_table(first, second).astype(jnp.bfloat16))
    factor = 1.0 / (math.sqrt(length) * 2.0 * length)
    skip_part = lax.dynamic_slice(skip_gain, (lax.axis_index("seq") * group,), (group,))

    product_kv = (key_in.astype(f32) * value_in.astype(f32)).astype(bf16)
    held = to_channels(jnp.stack([product_kv, filter_raw]))

    grad_mixed = lax.dot_general(
        gather_columns(cotangent),
        out_weight,
        (((1,), (1,)), ((), ())),
        preferred_element_type=f32,
    )
    grad_conv = (grad_mixed * queries.astype(f32)).astype(bf16)
    held_grad = to_channels(grad_conv[None])

    both = forward(held, outer, inner)
    zr, zi = both[:, 0, :, 0], both[:, 1, :, 0]
    hr, hi = both[:, 0, :, 1], both[:, 1, :, 1]
    conv = jnp.stack([hr * zr - hi * zi, hr * zi + hi * zr], axis=1).astype(bf16)
    conv = inverse(conv[:, :, :, None], outer_back, inner) * factor
    conv = (conv + skip_part * held[:1].astype(f32)).astype(bf16)
    convolved = to_positions(conv)[0].astype(f32)

    grad = forward(held_grad, outer, inner)
    gr, gi = grad[:, 0, :, 0], grad[:, 1, :, 0]
    back = jnp.stack([hr * gr + hi * gi, hr * gi - hi * gr], axis=1)
    taps = jnp.stack([zr * gr + zi * gi, zr * gi - zi * gr], axis=1)
    two = inverse(jnp.stack([back, taps], axis=3).astype(bf16), outer_back, inner) * factor
    back = two[0] + skip_part * held_grad[0].astype(f32)
    two = to_positions(jnp.stack([back, two[1]]).astype(bf16))

    gated_output = (queries.astype(f32) * convolved).astype(bf16)
    partial_terms = jnp.dot(gated_output, out_weight, preferred_element_type=f32)
    projected = scatter_columns(partial_terms).astype(bf16)
    grad_query = (grad_mixed * convolved).astype(bf16)
    grad_product = two[0].astype(f32)
    grad_key = (grad_product * value_in.astype(f32)).astype(bf16)
    grad_value = (grad_product * key_in.astype(f32)).astype(bf16)
    return (projected, grad_query, grad_key, grad_value, two[1])


def solution(mesh):
    placed = (
        P("seq", "ch"),
        P("seq", "ch"),
        P("seq", "ch"),
        P("seq", "ch"),
        P("ch"),
        P("ch", None),
        P("seq", "ch"),
    )
    return jax.shard_map(
        on_device,
        mesh=mesh,
        in_specs=placed,
        out_specs=(P("seq", "ch"),) * 5,
        check_vma=False,
    )
```

time: 691 us -> 239 us (0.35)
  matrix products: 267 us -> 42.7 us
  blocking collectives: 157 us -> 0 us
  waiting for transfers between devices: 159 us -> 97.9 us
  other arithmetic: 55.8 us -> 18.9 us
  starting transfers between devices: 5.92 us -> 35.7 us
  between operations: 14.4 us -> 1.07 us
  local copies, waits for them, and re-layouts: 27.8 us -> 40.9 us
    dot_general x14 -> x10, matrix products: 267 us -> 42.7 us  [the longest x2 9.5 us: forward(): jnp.einsum('fqgpb,fpbsc->fqgsc', inner, mid, preferred_element_type=f32)]
    all_to_all x1 -> x0, blocking collectives: 157 us -> none  [inverse(): lax.all_to_all(values, 'seq', split_axis=1, concat_axis=2, tiled=True)]
    reduce_scatter x1 -> x0, waiting for transfers between devices: 46.3 us -> none  [on_device(): lax.psum_scatter(partial_terms, 'ch', scatter_dimension=1, tiled=True)]
    ppermute x0 -> x2, waiting for transfers between devices: none -> 41.9 us  [shifted(): lax.ppermute(value, 'ch', [(i, (i + shift) % size) for i in range(size)])]
    all_gather x1 -> x0, waiting for transfers between devices: 34.6 us -> none  [on_device(): lax.all_gather(cotangent, 'ch', axis=1, tiled=True)]
    all_to_all x1 -> x4, starting transfers between devices: 5.67 us -> 31.1 us  [the longest x2 18.1 us: to_positions(): lax.all_to_all(parts, 'seq', split_axis=0, concat_axis=0, tiled=True)]
    all_to_all x1 -> x4, waiting for transfers between devices: 77 us -> 56 us  [the longest x2 49.2 us: to_channels(): lax.all_to_all(parts, 'seq', split_axis=0, concat_axis=0, tiled=True)]
    another operation x3, other arithmetic: 23.1 us -> 2.18 us  [the longest x1 1.71 us: on_device(): jnp.stack([hr * zr - hi * zi, hr * zi + hi * zr], axis=1).astype(bf16)]
  transfers between devices with their start and end apart: 3 -> 6, of which waited for: 3 -> 5; matrix products, arithmetic and copies ran while one was open for 2% -> 21% of each run, Pallas kernels for 0% -> 0%
where the time goes in v1:
time: 239 us; the launch traced here: 237 us
  waiting for transfers between devices  97.9 us (41%)
  matrix products  42.7 us (18%)
  local copies, waits for them, and re-layouts  40.9 us (17%)
  starting transfers between devices  35.7 us (15%)
  other arithmetic  18.9 us (8%)
    all_to_all x2, waiting for transfers between devices, to_channels(): lax.all_to_all(parts, 'seq', split_axis=0, concat_axis=0, tiled=True)  49.2 us
    ppermute x2, waiting for transfers between devices, shifted(): lax.ppermute(value, 'ch', [(i, (i + shift) % size) for i in range(size)])  41.9 us
    all_to_all x2, starting transfers between devices, to_positions(): lax.all_to_all(parts, 'seq', split_axis=0, concat_axis=0, tiled=True)  18.1 us
    unnamed x57, local copies, waits for them, and re-layouts  16.2 us
    all_to_all x2, starting transfers between devices, to_channels(): lax.all_to_all(parts, 'seq', split_axis=0, concat_axis=0, tiled=True)  13 us
    dot_general x2, matrix products, forward(): jnp.einsum('fqgpb,fpbsc->fqgsc', inner, mid, preferred_element_type=f32)  9.5 us
    dot_general x1, matrix products, on_device(): lax.dot_general(gather_columns(cotangent), out_weight, (((1,), (1,)), (()...  8.83 us
    dot_general x1, matrix products, on_device(): jnp.dot(gated_output, out_weight, preferred_element_type=f32)  8.41 us
  transfers between devices with their start and end apart: 6, of which 5 were waited for; matrix products, arithmetic and copies ran while one was open for 21% of the time, Pallas kernels for 0%

profile of v1, /device:TPU:0, one launch (start us, length us, event | category | flops | bytes accessed | tf_op | source)
XLA Modules:
  0.0 237.2 jit_solution(10760642446161468859)
XLA Ops:
  0.6 3.1 %collective-permute-start.1 = (bf16[256,2048]{1,0:T(8,128)(2,1)}, bf16[256,2048]{1,0:T(8,128)(2,1)S(1)}, u32[]{:S(2)}, u32[]{:S(2)}) collective-permute-start(bf16[256,2048]{1,0:T(8,128)(2,1)} %param.16), channel_id=1, source_target_pairs={{0,1},{1,0},{2,3},{3,2},{4,5},{5,4},{6,7},{7,6},{8,9},{9,8},{10,11... | collective-permute-start | bytes 3145736 | tf_op jit(solution)/shard_map/ppermute | solution.py:71
  3.7 1.6 broadcast_in_dim.2
  5.3 1.1 constant_dynamic-update-slice_fusion.1
  6.4 20.6 %collective-permute-done.1 = bf16[256,2048]{1,0:T(8,128)(2,1)S(1)} collective-permute-done((bf16[256,2048]{1,0:T(8,128)(2,1)}, bf16[256,2048]{1,0:T(8,128)(2,1)S(1)}, u32[]{:S(2)}, u32[]{:S(2)}) %collective-permute-start.1) | collective-permute-done | bytes 1048608 | tf_op jit(solution)/shard_map/ppermute | solution.py:71
  27.1 1.1 constant_dynamic-update-slice_fusion
  28.2 8.8 %fusion.55 = f32[256,2048]{1,0:T(8,128)S(1)} fusion(bf16[256,4096]{1,0:T(8,128)(2,1)} %constant_dynamic-update-slice_fusion, bf16[2048,4096]{1,0:T(8,128)(2,1)} %param.15), kind=kOutput, calls=%fused_computation.81 | convolution fusion | flops 4294967296 | bytes 20971520 | tf_op jit(solution)/shard_map/dot_general | solution.py:114
  37.0 0.3 fusion.50
  37.3 0.2 copy.146
  37.6 0.8 copy-done.4
  38.3 1.2 copy.176
  39.6 6.1 %all-to-all-start.2 = ((bf16[16,1,256,128]{3,2,1,0:T(8,128)(2,1)}), bf16[16,1,256,128]{3,2,1,0:T(8,128)(2,1)S(1)}, u32[]{:S(2)}, u32[]{:S(2)}) async-start(bf16[16,1,256,128]{3,2,1,0:T(8,128)(2,1)} %bitcast.228), calls=%async_computation.2 | async-start | bytes 2097152 | tf_op jit(solution)/shard_map/all_to_all | solution.py:57
  45.7 0.5 copy.75
  46.3 1.5 copy.76
  47.8 2.6 %copy.77 = bf16[256,2048]{0,1:T(8,128)(2,1)} copy(bf16[256,2048]{1,0:T(8,128)(2,1)} %param.13) | data formatting | bytes 2097152 | tf_op args[3]
  50.4 0.3 fusion.30
  50.7 0.9 copy-done.10
  51.8 1.4 copy.78
  53.3 15.3 %all-to-all-done.2 = bf16[16,1,256,128]{3,2,1,0:T(8,128)(2,1)S(1)} async-done(((bf16[16,1,256,128]{3,2,1,0:T(8,128)(2,1)}), bf16[16,1,256,128]{3,2,1,0:T(8,128)(2,1)S(1)}, u32[]{:S(2)}, u32[]{:S(2)}) %all-to-all-start.2) | async-done | bytes 1048608 | tf_op jit(solution)/shard_map/all_to_all | solution.py:57
  68.6 6.9 %all-to-all-start = ((bf16[16,2,256,128]{2,3,1,0:T(8,128)(2,1)}), bf16[16,2,256,128]{2,3,1,0:T(8,128)(2,1)}, u32[]{:S(2)}, u32[]{:S(2)}) async-start(bf16[16,2,256,128]{2,3,1,0:T(8,128)(2,1)} %copy.78), calls=%async_computation | async-start | bytes 4194304 | tf_op jit(solution)/shard_map/all_to_all | solution.py:57
  75.5 0.8 dynamic_slice.9
  76.2 1.0 convert_bitcast_fusion.1
  77.3 5.3 %convolution_bitcast_fusion = f32[65,2,64,1,128]{4,2,0,3,1:T(8,128)} fusion(bf16[65,2,64,2,64]{4,2,3,0,1:T(8,128)(2,1)} %constant.57, bf16[65,2,64,128]{3,0,1,2:T(8,128)(2,1)S(1)} %convert_bitcast_fusion.1), kind=kOutput, calls=%fused_computation.22 | convolution fusion | flops 272629760 | bytes 8519680 | tf_op jit(solution)/shard_map/fqgpb,fpbsc->fqgsc/dot_general | solution.py:42
  82.6 33.8 %all-to-all-done = bf16[16,2,256,128]{2,3,1,0:T(8,128)(2,1)} async-done(((bf16[16,2,256,128]{2,3,1,0:T(8,128)(2,1)}), bf16[16,2,256,128]{2,3,1,0:T(8,128)(2,1)}, u32[]{:S(2)}, u32[]{:S(2)}) %all-to-all-start) | async-done | bytes 2097184 | tf_op jit(solution)/shard_map/all_to_all | solution.py:57
  116.5 3.0 %copy.79 = bf16[16,2,256,128]{3,2,0,1:T(8,128)(2,1)S(1)} copy(bf16[16,2,256,128]{2,3,1,0:T(8,128)(2,1)} %all-to-all-done) | data formatting | bytes 4194304 | tf_op jit(solution)/shard_map/all_to_all | solution.py:57
  119.6 2.0 convert_bitcast_fusion
  121.5 4.2 %fusion.8 = f32[65,2,64,2,128]{4,2,3,1,0:T(8,128)S(1)} fusion(bf16[65,2,64,2,64,1]{4,2,3,5,1,0:T(8,128)(2,1)} %constant.53, bf16[65,2,64,2,128,1]{4,0,1,2,3,5:T(8,128)(2,1)S(1)} %convert_bitcast_fusion), kind=kOutput, calls=%fused_computation.13 | convolution fusion | flops 545259520 | bytes 14909440 | tf_op jit(solution)/shard_map/fqgpb,fpbsc->fqgsc/dot_general | solution.py:42
  125.7 2.6 %fusion.44 = (bf16[65,1,64,128]{3,2,0,1:T(8,128)(2,1)S(1)}, bf16[65,1,64,128]{3,2,0,1:T(8,128)(2,1)}, bf16[65,1,64,128]{3,2,0,1:T(8,128)(2,1)S(1)}, bf16[65,1,64,128]{3,2,0,1:T(8,128)(2,1)S(1)}) fusion(f32[65,2,64,1,128]{4,2,0,3,1:T(8,128)S(1)} %bitcast.230, f32[65,2,64,2,128]{4,2,3,1,0:T(8,128)S(1)} %fusion.8), kind=kLoop, calls=%fused_computation.67 | loop fusion | flops 8519680 | bytes 17039360 | tf_op jit(solution)/shard_map/add | solution.py:133
  128.3 2.0 fusion.49
  130.3 1.0 fusion.47
  131.3 1.7 maximum_bitcast_fusion.1
  133.1 1.3 fusion.39
  134.4 1.5 fusion.37
  135.9 1.2 copy.90
  137.2 1.3 fusion.36
  138.5 2.4 %copy.91 = bf16[16,1,256,128]{2,3,1,0:T(8,128)(2,1)} copy(bf16[16,1,256,128]{3,2,0,1:T(8,128)(2,1)} %fusion.36) | data formatting | bytes 2097152 | tf_op jit(solution)/shard_map/convert_element_type | solution.py:128
  140.9 11.3 %all-to-all-start.1 = ((bf16[16,1,256,128]{2,3,1,0:T(8,128)(2,1)}), bf16[16,1,256,128]{2,3,1,0:T(8,128)(2,1)}, u32[]{:S(2)}, u32[]{:S(2)}) async-start(bf16[16,1,256,128]{2,3,1,0:T(8,128)(2,1)} %copy.91), calls=%async_computation.1 | async-start | bytes 2097152 | tf_op jit(solution)/shard_map/all_to_all | solution.py:65
  152.4 1.4 copy-done.13
  153.8 5.5 %fusion.2 = bf16[65,2,64,2,128]{4,2,1,3,0:T(8,128)(2,1)S(1)} fusion(bf16[65,2,64,2,64,1]{4,2,1,3,5,0:T(8,128)(2,1)} %constant.60, bf16[65,2,64,1,128]{4,2,0,1,3:T(8,128)(2,1)S(1)} %maximum_bitcast_fusion.3, bf16[65,2,64,1,128]{4,2,0,1,3:T(8,128)(2,1)S(1)} %copy-done.13), kind=kOutput, calls=%fused_computation.4 | convolution fusion | flops 549519360 | bytes 10649600 | tf_op jit(solution)/shard_map/fqgpb,fqgsc->fpbsc/dot_general | solution.py:47
  159.3 4.6 %fusion.7 = f32[2,64,64,128]{3,1,0,2:T(8,128)S(1)} fusion(bf16[2,65,64,1,1]{1,2,0,4,3:T(8,128)(2,1)S(1)} %copy-done.17, bf16[65,2,64,2,128]{4,2,1,3,0:T(8,128)(2,1)S(1)} %fusion.2), kind=kOutput, calls=%fused_computation.12 | convolution fusion | flops 273678336 | bytes 8470784 | tf_op jit(solution)/shard_map/pfa,fpbsc->sabc/dot_general | solution.py:49
  163.9 0.2 slice.60
  164.1 0.2 slice.155
  164.4 1.2 copy.103
  165.6 0.7 copy.105
  166.3 0.3 fusion.34
  166.8 1.5 copy.106
  168.2 6.9 %all-to-all-done.1 = bf16[16,1,256,128]{2,3,1,0:T(8,128)(2,1)} async-done(((bf16[16,1,256,128]{2,3,1,0:T(8,128)(2,1)}), bf16[16,1,256,128]{2,3,1,0:T(8,128)(2,1)}, u32[]{:S(2)}, u32[]{:S(2)}) %all-to-all-start.1) | async-done | bytes 1048608 | tf_op jit(solution)/shard_map/all_to_all | solution.py:65
  175.1 6.9 %all-to-all-start.3 = ((bf16[16,2,256,128]{3,2,1,0:T(8,128)(2,1)}), bf16[16,2,256,128]{3,2,1,0:T(8,128)(2,1)}, u32[]{:S(2)}, u32[]{:S(2)}) async-start(bf16[16,2,256,128]{3,2,1,0:T(8,128)(2,1)} %copy.106), calls=%async_computation.3 | async-start | bytes 4194304 | tf_op jit(solution)/shard_map/all_to_all | solution.py:65
  181.9 2.8 %convert_element_type.163 = f32[16,1,256,128]{2,3,1,0:T(8,128)} convert(bf16[16,1,256,128]{2,3,1,0:T(8,128)(2,1)} %all-to-all-done.1) | non-fusion elementwise | flops 524288 | bytes 3145728 | tf_op jit(solution)/shard_map/convert_element_type | solution.py:129
  184.8 1.9 copy.135
  186.7 1.3 copy-done.6
  188.0 8.4 %fusion.51 = f32[256,4096]{1,0:T(8,128)S(1)} fusion(bf16[2048,4096]{1,0:T(8,128)(2,1)} %param.15, f32[256,2048]{1,0:T(8,128)S(1)} %copy.135, bf16[256,2048]{1,0:T(8,128)(2,1)} %param.10), kind=kOutput, calls=%fused_computation.74 | convolution fusion | flops 4296540160 | bytes 24117248 | tf_op jit(solution)/shard_map/dot_general | solution.py:140
  196.5 2.0 copy-done.11
  198.5 1.1 dynamic-slice_convert_fusion
  199.6 1.5 collective-permute-start
  201.1 2.9 %multiply_convert_fusion = bf16[256,2048]{1,0:T(8,128)(2,1)} fusion(f32[256,2048]{1,0:T(8,128)S(1)} %copy-done.5, f32[256,2048]{1,0:T(8,128)} %copy-done.6), kind=kLoop, calls=%fused_computation.63 | loop fusion | flops 1048576 | bytes 5242880 | tf_op jit(solution)/shard_map/convert_element_type | solution.py:142
  204.0 21.3 %collective-permute-done = bf16[256,2048]{1,0:T(8,128)(2,1)} collective-permute-done((bf16[256,2048]{1,0:T(8,128)(2,1)}, bf16[256,2048]{1,0:T(8,128)(2,1)}, u32[]{:S(2)}, u32[]{:S(2)}) %collective-permute-start) | collective-permute-done | bytes 1048608 | tf_op jit(solution)/shard_map/ppermute | solution.py:71
  225.3 2.5 %add_convert_fusion.1 = bf16[256,2048]{1,0:T(8,128)(2,1)} fusion(bf16[256,2048]{1,0:T(8,128)(2,1)} %collective-permute-done, f32[256,4096]{1,0:T(8,128)S(1)} %copy-done.12, s32[]{:T(128)S(6)} %select_n.27), kind=kLoop, calls=%fused_computation.64 | loop fusion | flops 1572864 | bytes 4194308 | tf_op jit(solution)/shard_map/convert_element_type | solution.py:141
  227.9 2.9 %copy.107 = bf16[16,2,256,128]{2,3,0,1:T(8,128)(2,1)S(1)} copy(bf16[16,2,256,128]{3,2,1,0:T(8,128)(2,1)} %all-to-all-done.3) | data formatting | bytes 4194304 | tf_op jit(solution)/shard_map/all_to_all | solution.py:65
  230.7 1.1 fusion.54
  231.8 0.5 copy-done.1
  232.3 0.6 fusion.32
  232.9 1.4 copy.108
  234.4 1.4 copy.109
  235.8 1.4 copy.110
  (50 shorter events, 0.7 us)
Async XLA Ops:
  0.6 4.7 %copy-start.14 = (bf16[256,2048]{1,0:T(8,128)(2,1)S(1)}, bf16[256,2048]{1,0:T(8,128)(2,1)}, u32[]{:S(2)}) copy-start(bf16[256,2048]{1,0:T(8,128)(2,1)} %param.16) | copy-start | bytes 3145732
  0.6 26.4 %collective-permute-start.1 = (bf16[256,2048]{1,0:T(8,128)(2,1)}, bf16[256,2048]{1,0:T(8,128)(2,1)S(1)}, u32[]{:S(2)}, u32[]{:S(2)}) collective-permute-start(bf16[256,2048]{1,0:T(8,128)(2,1)} %param.16), channel_id=1, source_target_pairs={{0,1},{1,0},{2,3},{3,2},{4,5},{5,4},{6,7},{7,6},{8,9},{9,8},{10,11... | collective-permute-start | bytes 3145736 | tf_op jit(solution)/shard_map/ppermute | solution.py:71
  28.2 8.8 %copy-start.16 = (bf16[256,2048]{1,0:T(8,128)(2,1)S(1)}, bf16[256,2048]{1,0:T(8,128)(2,1)}, u32[]{:S(2)}) copy-start(bf16[256,2048]{1,0:T(8,128)(2,1)} %param.10) | copy-start | bytes 3145732
  37.0 1.3 copy-start.4
  38.3 7.4 %copy-start.15 = (bf16[256,2048]{1,0:T(8,128)(2,1)S(1)}, bf16[256,2048]{1,0:T(8,128)(2,1)}, u32[]{:S(2)}) copy-start(bf16[256,2048]{1,0:T(8,128)(2,1)} %param.11) | copy-start | bytes 3145732
  39.6 29.0 %all-to-all-start.2 = ((bf16[16,1,256,128]{3,2,1,0:T(8,128)(2,1)}), bf16[16,1,256,128]{3,2,1,0:T(8,128)(2,1)S(1)}, u32[]{:S(2)}, u32[]{:S(2)}) async-start(bf16[16,1,256,128]{3,2,1,0:T(8,128)(2,1)} %bitcast.228), calls=%async_computation.2 | async-start | bytes 2097152 | tf_op jit(solution)/shard_map/all_to_all | solution.py:57
  47.8 2.9 %copy-start = (bf16[256,2048]{0,1:T(8,128)(2,1)}, bf16[256,2048]{0,1:T(8,128)(2,1)S(1)}, u32[]{:S(2)}) copy-start(bf16[256,2048]{0,1:T(8,128)(2,1)S(1)} %copy.76) | copy-start | bytes 3145732
  50.4 1.2 copy-start.10
  53.3 23.0 %copy-start.20 = (bf16[2,65,64,1]{1,2,0,3:T(8,128)(2,1)S(1)}, bf16[2,65,64,1]{1,2,0,3:T(8,128)(2,1)}, u32[]{:S(2)}) copy-start(bf16[2,65,64,1]{1,2,0,3:T(8,128)(2,1)} %constant.58) | copy-start | bytes 49924
  68.6 8.7 %copy-start.2 = (bf16[16,1,256,128]{3,2,1,0:T(8,128)(2,1)}, bf16[16,1,256,128]{3,2,1,0:T(8,128)(2,1)S(1)}, u32[]{:S(2)}) copy-start(bf16[16,1,256,128]{3,2,1,0:T(8,128)(2,1)S(1)} %all-to-all-done.2) | copy-start | bytes 3145732
  68.6 47.9 %all-to-all-start = ((bf16[16,2,256,128]{2,3,1,0:T(8,128)(2,1)}), bf16[16,2,256,128]{2,3,1,0:T(8,128)(2,1)}, u32[]{:S(2)}, u32[]{:S(2)}) async-start(bf16[16,2,256,128]{2,3,1,0:T(8,128)(2,1)} %copy.78), calls=%async_computation | async-start | bytes 4194304 | tf_op jit(solution)/shard_map/all_to_all | solution.py:57
  82.6 36.9 %copy-start.19 = (bf16[2,65,64,1,1]{1,2,0,4,3:T(8,128)(2,1)S(1)}, bf16[2,65,64,1,1]{1,2,0,4,3:T(8,128)(2,1)}, u32[]{:S(2)}) copy-start(bf16[2,65,64,1,1]{1,2,0,4,3:T(8,128)(2,1)} %constant.54) | copy-start | bytes 49924
  119.5 6.1 %slice-start = ((s8[4259840]{0:T(1024)(128)(4,1)}), s8[4194304]{0:T(1024)(128)(4,1)S(1)}, s32[]{:S(2)}) async-start(s8[4259840]{0:T(1024)(128)(4,1)} %bitcast.229), calls=%async_computation.4 | async-start | bytes 8388608
  121.5 4.2 %slice-start.1 = ((s8[4259840]{0:T(1024)(128)(4,1)}), s8[65536]{0:T(1024)(128)(4,1)S(1)}, s32[]{:S(2)}) async-start(s8[4259840]{0:T(1024)(128)(4,1)} %bitcast.229), calls=%async_computation.5 | async-start | bytes 131072
  128.3 4.7 %slice-start.2 = ((s8[4259840]{0:T(1024)(128)(4,1)}), s8[65536]{0:T(1024)(128)(4,1)S(1)}, s32[]{:S(2)}) async-start(s8[4259840]{0:T(1024)(128)(4,1)} %bitcast.238), calls=%async_computation.6 | async-start | bytes 131072
  130.3 2.8 %slice-start.3 = ((s8[4259840]{0:T(1024)(128)(4,1)}), s8[4194304]{0:T(1024)(128)(4,1)S(1)}, s32[]{:S(2)}) async-start(s8[4259840]{0:T(1024)(128)(4,1)} %bitcast.238), calls=%async_computation.7 | async-start | bytes 8388608
  133.1 1.4 copy-start.18
  138.5 13.7 %copy-start.7 = (bf16[65,1,64,128]{3,2,0,1:T(8,128)(2,1)S(1)}, bf16[65,1,64,128]{3,2,0,1:T(8,128)(2,1)}, u32[]{:S(2)}) copy-start(bf16[65,1,64,128]{3,2,0,1:T(8,128)(2,1)} %get-tuple-element.16) | copy-start | bytes 3194884
  138.5 13.7 %copy-start.8 = (bf16[65,1,64,128]{3,2,0,1:T(8,128)(2,1)S(1)}, bf16[65,1,64,128]{3,2,0,1:T(8,128)(2,1)}, u32[]{:S(2)}) copy-start(bf16[65,1,64,128]{3,2,0,1:T(8,128)(2,1)} %fusion.49) | copy-start | bytes 3194884
  140.9 34.2 %all-to-all-start.1 = ((bf16[16,1,256,128]{2,3,1,0:T(8,128)(2,1)}), bf16[16,1,256,128]{2,3,1,0:T(8,128)(2,1)}, u32[]{:S(2)}, u32[]{:S(2)}) async-start(bf16[16,1,256,128]{2,3,1,0:T(8,128)(2,1)} %copy.91), calls=%async_computation.1 | async-start | bytes 2097152 | tf_op jit(solution)/shard_map/all_to_all | solution.py:65
  152.2 1.6 copy-start.13
  153.8 5.5 %copy-start.17 = (bf16[2,65,64,1,1]{1,2,0,4,3:T(8,128)(2,1)S(1)}, bf16[2,65,64,1,1]{1,2,0,4,3:T(8,128)(2,1)}, u32[]{:S(2)}) copy-start(bf16[2,65,64,1,1]{1,2,0,4,3:T(8,128)(2,1)} %constant.61) | copy-start | bytes 49924
  164.3 1.9 copy-start.3
  175.1 52.8 %all-to-all-start.3 = ((bf16[16,2,256,128]{3,2,1,0:T(8,128)(2,1)}), bf16[16,2,256,128]{3,2,1,0:T(8,128)(2,1)}, u32[]{:S(2)}, u32[]{:S(2)}) async-start(bf16[16,2,256,128]{3,2,1,0:T(8,128)(2,1)} %copy.106), calls=%async_computation.3 | async-start | bytes 4194304 | tf_op jit(solution)/shard_map/all_to_all | solution.py:65
  186.7 1.4 copy-start.6
  196.5 2.0 copy-start.11
  198.5 2.6 %copy-start.5 = (f32[256,2048]{1,0:T(8,128)S(1)}, f32[256,2048]{1,0:T(8,128)}, u32[]{:S(2)}) copy-start(f32[256,2048]{1,0:T(8,128)} %copy-done.4) | copy-start | bytes 6291460
  199.6 25.7 %collective-permute-start = (bf16[256,2048]{1,0:T(8,128)(2,1)}, bf16[256,2048]{1,0:T(8,128)(2,1)}, u32[]{:S(2)}, u32[]{:S(2)}) collective-permute-start(bf16[256,2048]{1,0:T(8,128)(2,1)} %dynamic-slice_convert_fusion), channel_id=1, source_target_pairs={{0,1},{1,0},{2,3},{3,2},{4,5},{5,4},{6,7},{7,6},{8,9},{9,8},{10,11... | collective-permute-start | bytes 3145736 | tf_op jit(solution)/shard_map/ppermute | solution.py:71
  201.1 24.2 %copy-start.12 = (f32[256,4096]{1,0:T(8,128)S(1)}, f32[256,4096]{1,0:T(8,128)}, u32[]{:S(2)}) copy-start(f32[256,4096]{1,0:T(8,128)} %copy-done.11) | copy-start | bytes 12582916
  230.7 1.6 copy-start.1
  232.9 2.9 %copy-start.9 = (bf16[1,256,16,128]{1,3,2,0:T(8,128)(2,1)S(1)}, bf16[1,256,16,128]{1,3,2,0:T(8,128)(2,1)}, u32[]{:S(2)}) copy-start(bf16[1,256,16,128]{1,3,2,0:T(8,128)(2,1)} %get-tuple-element.19) | copy-start | bytes 3145732

commit v2 on v1

v2 whole, which is shorter than its diff:
```python
import math

import jax
import jax.numpy as jnp
import numpy as np
from jax import lax
from jax.experimental import pallas as pl
from jax.sharding import PartitionSpec as P


bf16 = jnp.bfloat16
f32 = jnp.float32


def split_period(period):
    second = 1 << ((period.bit_length() - 1) // 2)
    return period // second, second


def outer_table(first):
    f1 = np.arange(first // 2 + 1)[:, None]
    a = np.arange(first // 2)[None, :]
    angles = (f1 * a % first) * (2.0 * math.pi / first)
    return np.stack([np.cos(angles), -np.sin(angles)])


def inner_table(first, second):
    period = first * second
    f1 = np.arange(first // 2 + 1)[:, None, None]
    f2 = np.arange(second)[None, :, None]
    b = np.arange(second)[None, None, :]
    angles = (b * (f1 + first * f2) % period) * (2.0 * math.pi / period)
    cosine, sine = np.cos(angles), np.sin(angles)
    top = np.concatenate([cosine, sine], axis=2)
    bottom = np.concatenate([-sine, cosine], axis=2)
    return np.concatenate([top, bottom], axis=1)


def forward(signal, outer, inner):
    count, _, width = signal.shape
    second = inner.shape[2] // 2
    pieces = signal.reshape(count, outer.shape[2], second, width)
    mid = jnp.einsum("pfa,sabc->fpbsc", outer, pieces, preferred_element_type=f32)
    mid = mid.astype(bf16).reshape(-1, 2 * second, count, width)
    return jnp.einsum("fxy,fysc->fxsc", inner, mid, preferred_element_type=f32)


def inverse(spectra, outer, inner):
    freqs, double, count, width = spectra.shape
    mid = jnp.einsum("fxy,fxsc->fysc", inner, spectra, preferred_element_type=f32)
    mid = mid.astype(bf16).reshape(freqs, 2, double // 2, count, width)
    out = jnp.einsum("pfa,fpbsc->sabc", outer, mid, preferred_element_type=f32)
    return out.reshape(count, -1, width)


def exchange(value):
    return lax.all_to_all(value, "seq", split_axis=0, concat_axis=0, tiled=True)


def grouped(body, wide, tall, wide_out, tall_out):
    rows = (wide[0] if wide else tall[0]).shape[0 if wide else 2]
    width = wide[0].shape[1] // lax.axis_size("seq") if wide else tall[0].shape[3]
    groups = lax.axis_size("seq")
    if width % 128:
        wide_tiles = [
            [v[:, i * width : (i + 1) * width] for v in wide] for i in range(groups)
        ]
        results = [
            body(wide_tiles[i], [[v[i, k] for k in range(v.shape[1])] for v in tall])
            for i in range(groups)
        ]
        outs = [
            jnp.concatenate([r[0][j] for r in results], axis=1).astype(t)
            for j, t in enumerate(wide_out)
        ]
        outs += [
            jnp.stack([jnp.stack(r[1][j]) for r in results]).astype(t)
            for j, (_, t) in enumerate(tall_out)
        ]
        return outs
    step = math.gcd(groups, 4)

    def kernel(*refs):
        wide_in = refs[: len(wide)]
        tall_in = refs[len(wide) : len(wide) + len(tall)]
        outs = refs[len(wide) + len(tall) :]
        for i in range(step):
            lanes = slice(i * width, (i + 1) * width)
            flat, stacked = body(
                [r[:, lanes] for r in wide_in],
                [[r[i, k] for k in range(r.shape[1])] for r in tall_in],
            )
            for ref, value in zip(outs, flat):
                ref[:, lanes] = value.astype(ref.dtype)
            for ref, kinds in zip(outs[len(flat) :], stacked):
                for k, value in enumerate(kinds):
                    ref[i, k] = value.astype(ref.dtype)

    flat_spec = pl.BlockSpec((rows, step * width), lambda i: (0, i))

    def tall_spec(kinds):
        return pl.BlockSpec((step, kinds, rows, width), lambda i: (i, 0, 0, 0))

    shapes = [jax.ShapeDtypeStruct((rows, groups * width), t) for t in wide_out]
    shapes += [jax.ShapeDtypeStruct((groups, n, rows, width), t) for n, t in tall_out]
    moved = sum(v.size * v.dtype.itemsize for v in [*wide, *tall])
    moved += sum(math.prod(v.shape) * v.dtype.itemsize for v in shapes)
    return pl.pallas_call(
        kernel,
        grid=(groups // step,),
        in_specs=[flat_spec] * len(wide) + [tall_spec(v.shape[1]) for v in tall],
        out_specs=[flat_spec] * len(wide_out) + [tall_spec(n) for n, _ in tall_out],
        out_shape=shapes,
        cost_estimate=pl.CostEstimate(
            flops=rows * groups * width * 8, bytes_accessed=moved, transcendentals=0
        ),
    )(*wide, *tall)


def pack_inputs(tiles, _):
    key, value, taps = tiles
    product = key.astype(f32) * value.astype(f32)
    return [], [[product.astype(bf16), taps]]


def pack_gradient(tiles, _):
    mixed, queries = tiles
    return [], [[mixed * queries.astype(f32)]]


def unpack_convolved(tiles, tall):
    mixed, queries = tiles
    convolved = tall[0][0].astype(f32)
    return [queries.astype(f32) * convolved, mixed * convolved], []


def unpack_gradients(tiles, tall):
    key, value = tiles
    back, taps = tall[0]
    back = back.astype(f32)
    return [back * value.astype(f32), back * key.astype(f32), taps], []


def shifted(value, shift):
    size = lax.axis_size("ch")
    return lax.ppermute(value, "ch", [(i, (i + shift) % size) for i in range(size)])


def gather_columns(value):
    size, me = lax.axis_size("ch"), lax.axis_index("ch")
    rows, width = value.shape
    full = jnp.zeros((rows, size * width), value.dtype)
    for shift in range(size):
        part = shifted(value, shift) if shift else value
        owner = (me - shift + size) % size
        full = lax.dynamic_update_slice(full, part, (0, owner * width))
    return full


def scatter_columns(value):
    size, me = lax.axis_size("ch"), lax.axis_index("ch")
    rows, width = value.shape[0], value.shape[1] // size
    total = lax.dynamic_slice(value, (0, me * width), (rows, width))
    for shift in range(1, size):
        target = (me + shift) % size
        part = lax.dynamic_slice(value, (0, target * width), (rows, width)).astype(bf16)
        total = total + shifted(part, shift).astype(f32)
    return total


def on_device(queries, key_in, value_in, filter_raw, skip_gain, out_weight, cotangent):
    local_rows, local_width = queries.shape
    seq_devices = lax.axis_size("seq")
    length = local_rows * seq_devices
    group = local_width // seq_devices
    first, second = split_period(2 * length)
    table = outer_table(first)
    weight = np.full((first // 2 + 1, 1), 2.0)
    weight[0] = weight[-1] = 1.0
    outer = jnp.asarray(table, bf16)
    outer_back = jnp.asarray(table * weight, bf16)
    inner = lax.optimization_barrier(jnp.asarray(inner_table(first, second), bf16))
    factor = 1.0 / (math.sqrt(length) * 2.0 * length)
    skip_part = lax.dynamic_slice(skip_gain, (lax.axis_index("seq") * group,), (group,))

    def held_form(parts):
        return parts.transpose(1, 0, 2, 3).reshape(parts.shape[1], length, group)

    def sent_form(values):
        kinds = values.shape[0]
        return values.reshape(kinds, seq_devices, local_rows, group).transpose(1, 0, 2, 3)

    (sent,) = grouped(pack_inputs, [key_in, value_in, filter_raw], [], [], [(2, bf16)])
    got = exchange(sent)
    held = held_form(got)

    gathered = gather_columns(cotangent)
    grad_mixed = lax.dot_general(
        gathered, out_weight, (((1,), (1,)), ((), ())), preferred_element_type=f32
    )
    (sent,) = grouped(pack_gradient, [grad_mixed, queries], [], [], [(1, bf16)])
    got = exchange(sent)
    held_grad = held_form(got)

    both = forward(held, outer, inner)
    zr, zi = both[:, :second, 0], both[:, second:, 0]
    hr, hi = both[:, :second, 1], both[:, second:, 1]
    conv = jnp.concatenate([hr * zr - hi * zi, hr * zi + hi * zr], axis=1).astype(bf16)
    conv = inverse(conv[:, :, None], outer_back, inner) * factor
    conv = (conv + skip_part * held[:1].astype(f32)).astype(bf16)
    convolved = exchange(sent_form(conv))

    grad = forward(held_grad, outer, inner)
    zr, zi, hr, hi = lax.optimization_barrier((zr, zi, hr, hi))
    gr, gi = grad[:, :second, 0], grad[:, second:, 0]
    back = jnp.concatenate([hr * gr + hi * gi, hr * gi - hi * gr], axis=1)
    taps = jnp.concatenate([zr * gr + zi * gi, zr * gi - zi * gr], axis=1)
    two = inverse(jnp.stack([back, taps], axis=2).astype(bf16), outer_back, inner) * factor
    back = two[0] + skip_part * held_grad[0].astype(f32)
    two = sent_form(jnp.stack([back, two[1]]).astype(bf16))
    two = exchange(two)

    gated_output, grad_query = grouped(
        unpack_convolved, [grad_mixed, queries], [convolved], [bf16, bf16], []
    )
    partial_terms = jnp.dot(gated_output, out_weight, preferred_element_type=f32)
    projected = scatter_columns(partial_terms).astype(bf16)
    grad_key, grad_value, grad_filter = grouped(
        unpack_gradients, [key_in, value_in], [two], [bf16, bf16, bf16], []
    )
    return (projected, grad_query, grad_key, grad_value, grad_filter)


def solution(mesh):
    placed = (
        P("seq", "ch"),
        P("seq", "ch"),
        P("seq", "ch"),
        P("seq", "ch"),
        P("ch"),
        P("ch", None),
        P("seq", "ch"),
    )
    return jax.shard_map(
        on_device,
        mesh=mesh,
        in_specs=placed,
        out_specs=(P("seq", "ch"),) * 5,
        check_vma=False,
    )
```

time: 239 us -> 229 us (0.958)
  local copies, waits for them, and re-layouts: 40.9 us -> 18.4 us
  Pallas kernels: 0 us -> 16.7 us
  matrix products: 42.7 us -> 33.3 us
  waiting for transfers between devices: 97.9 us -> 106 us
  other arithmetic: 18.9 us -> 14.3 us
    pallas_call x0 -> x4, Pallas kernels: none -> 16.7 us  [grouped(): pl.pallas_call(kernel, grid=(groups // step,), in_specs=[flat_spec] * len...]
    unnamed x57 -> x16, local copies, waits for them, and re-layouts: 16.2 us -> 4.33 us
    dot_general x5, matrix products: 25.2 us -> 15.8 us  [the longest x1 9.45 us: on_device(): lax.dot_general(gathered, out_weight, (((1,), (1,)), ((), ())), preferred...]
    convert_element_type x4 -> x0, other arithmetic: 6.62 us -> none  [the longest x1 2.95 us: on_device(): grad_query = (grad_mixed * convolved).astype(bf16)]
    another operation x3 -> x4, other arithmetic: 2.18 us -> 8.64 us  [the longest x1 1.71 us: on_device(): jnp.stack([hr * zr - hi * zi, hr * zi + hi * zr], axis=1).astype(bf16)]
    ppermute x2, waiting for transfers between devices: 41.9 us -> 47.3 us  [shifted(): lax.ppermute(value, 'ch', [(i, (i + shift) % size) for i in range(size)])]
    all_to_all x2 -> x1, local copies, waits for them, and re-layouts: 5.89 us -> 1.73 us  [exchange(): return lax.all_to_all(value, 'seq', split_axis=0, concat_axis=0, tiled=True)]
    add x2 -> x0, other arithmetic: 3.63 us -> none  [the longest x1 2.6 us: on_device(): back = jnp.stack([hr * gr + hi * gi, hr * gi - hi * gr], axis=1)]
  transfers between devices with their start and end apart: 6 -> 6, of which waited for: 5 -> 5; matrix products, arithmetic and copies ran while one was open for 21% -> 16% of each run, Pallas kernels for 0% -> 4%
where the time goes in v2:
time: 229 us; the launch traced here: 225 us
  waiting for transfers between devices  106 us (46%)
  starting transfers between devices  35.8 us (16%)
  matrix products  33.3 us (15%)
  local copies, waits for them, and re-layouts  18.4 us (8%)
  Pallas kernels  16.7 us (7%)
  other arithmetic  14.3 us (6%)
    all_to_all x4, waiting for transfers between devices, exchange(): return lax.all_to_all(value, 'seq', split_axis=0, concat_axis=0, tiled=True)  58.8 us
    ppermute x2, waiting for transfers between devices, shifted(): lax.ppermute(value, 'ch', [(i, (i + shift) % size) for i in range(size)])  47.3 us
    all_to_all x4, starting transfers between devices, exchange(): return lax.all_to_all(value, 'seq', split_axis=0, concat_axis=0, tiled=True)  31.2 us
    pallas_call x4, Pallas kernels, grouped(): pl.pallas_call(kernel, grid=(groups // step,), in_specs=[flat_spec] * len...  16.7 us
    dot_general x1, matrix products, on_device(): lax.dot_general(gathered, out_weight, (((1,), (1,)), ((), ())), preferred...  9.45 us
    dot_general x1, matrix products, on_device(): jnp.dot(gated_output, out_weight, preferred_element_type=f32)  8.42 us
    another operation x3, other arithmetic  7.8 us
    dot_general x2, matrix products, inverse(): out = jnp.einsum('pfa,fpbsc->sabc', outer, mid, preferred_element_type=f32)  6.09 us
  transfers between devices with their start and end apart: 6, of which 5 were waited for; matrix products, arithmetic and copies ran while one was open for 16% of the time, Pallas kernels for 4%

profile of v2, /device:TPU:0, one launch (start us, length us, event | category | flops | bytes accessed | tf_op | source)
XLA Modules:
  0.0 225.4 jit_solution(5884679773602769067)
XLA Ops:
  0.6 0.0 copy-start.3
  0.6 3.1 %collective-permute-start = (bf16[256,2048]{1,0:T(8,128)(2,1)}, bf16[256,2048]{1,0:T(8,128)(2,1)}, u32[]{:S(2)}, u32[]{:S(2)}) collective-permute-start(bf16[256,2048]{1,0:T(8,128)(2,1)} %param.16), channel_id=1, source_target_pairs={{0,1},{1,0},{2,3},{3,2},{4,5},{5,4},{6,7},{7,6},{8,9},{9,8},{10,11... | collective-permute-start | bytes 3145736 | tf_op jit(solution)/shard_map/ppermute | solution.py:146
  3.7 0.2 broadcast_in_dim.2
  3.9 0.0 copy-done.3
  3.9 0.1 constant_dynamic-update-slice_fusion.1
  4.1 23.1 %collective-permute-done = bf16[256,2048]{1,0:T(8,128)(2,1)} collective-permute-done((bf16[256,2048]{1,0:T(8,128)(2,1)}, bf16[256,2048]{1,0:T(8,128)(2,1)}, u32[]{:S(2)}, u32[]{:S(2)}) %collective-permute-start) | collective-permute-done | bytes 1048608 | tf_op jit(solution)/shard_map/ppermute | solution.py:146
  27.2 1.3 constant_dynamic-update-slice_fusion
  28.5 9.4 %fusion.32.refs_0_ = f32[256,2048]{1,0:T(8,128)} fusion(bf16[256,4096]{1,0:T(8,128)(2,1)S(1)} %constant_dynamic-update-slice_fusion, bf16[2048,4096]{1,0:T(8,128)(2,1)} %param.15), kind=kOutput, calls=%fused_computation.54 | convolution fusion | flops 4294967296 | bytes 20971520 | tf_op jit(solution)/shard_map/dot_general | solution.py:198
  37.9 3.8 %shard_map.139 = bf16[16,1,256,128]{3,2,1,0:T(8,128)(2,1)} custom-call(f32[256,2048]{1,0:T(8,128)} %fusion.32.refs_0_, bf16[256,2048]{1,0:T(8,128)(2,1)} %refs_1_.6), custom_call_target="tpu_custom_call" | custom-call | flops 4194304 | bytes 4194304 | tf_op jit(solution)/shard_map/pallas_call | solution.py:108
  41.8 6.1 %all-to-all-start.2 = ((bf16[16,1,256,128]{3,2,1,0:T(8,128)(2,1)}), bf16[16,1,256,128]{3,2,1,0:T(8,128)(2,1)S(1)}, u32[]{:S(2)}, u32[]{:S(2)}) async-start(bf16[16,1,256,128]{3,2,1,0:T(8,128)(2,1)} %shard_map.139), calls=%async_computation.2 | async-start | bytes 2097152 | tf_op jit(solution)/shard_map/all_to_all | solution.py:57
  47.9 4.1 %shard_map.137 = bf16[16,2,256,128]{3,2,1,0:T(8,128)(2,1)} custom-call(bf16[256,2048]{1,0:T(8,128)(2,1)} %refs_0_.3, bf16[256,2048]{1,0:T(8,128)(2,1)} %refs_1_.7, bf16[256,2048]{1,0:T(8,128)(2,1)} %refs_2_.1), custom_call_target="tpu_custom_call" | custom-call | flops 4194304 | bytes 5242880 | tf_op jit(solution)/shard_map/pallas_call | solution.py:108
  52.0 0.0 copy-start.7
  52.0 18.7 %all-to-all-done.2 = bf16[16,1,256,128]{3,2,1,0:T(8,128)(2,1)S(1)} async-done(((bf16[16,1,256,128]{3,2,1,0:T(8,128)(2,1)}), bf16[16,1,256,128]{3,2,1,0:T(8,128)(2,1)S(1)}, u32[]{:S(2)}, u32[]{:S(2)}) %all-to-all-start.2) | async-done | bytes 1048608 | tf_op jit(solution)/shard_map/all_to_all | solution.py:57
  70.8 7.0 %all-to-all-start = ((bf16[16,2,256,128]{3,2,1,0:T(8,128)(2,1)}), bf16[16,2,256,128]{3,2,1,0:T(8,128)(2,1)}, u32[]{:S(2)}, u32[]{:S(2)}) async-start(bf16[16,2,256,128]{3,2,1,0:T(8,128)(2,1)} %shard_map.137), calls=%async_computation | async-start | bytes 4194304 | tf_op jit(solution)/shard_map/all_to_all | solution.py:57
  77.8 0.8 dynamic_slice.9
  78.6 0.0 copy-done.7
  78.6 1.0 convert_bitcast_fusion.1
  79.6 0.0 copy-start
  79.6 0.6 copy.54
  80.2 1.0 copy-done
  81.2 2.9 %convolution_bitcast_fusion = f32[65,128,1,128]{3,1,0,2:T(8,128)} fusion(bf16[65,128,128]{1,2,0:T(8,128)(2,1)S(1)} %copy-done, bf16[65,128,128]{2,1,0:T(8,128)(2,1)S(1)} %bitcast.146), kind=kOutput, calls=%fused_computation.12 | convolution fusion | flops 272629760 | bytes 8519680 | tf_op jit(solution)/shard_map/fxy,fysc->fxsc/dot_general | solution.py:45
  84.1 0.0 copy-start.6
  84.1 34.6 %all-to-all-done = bf16[16,2,256,128]{3,2,1,0:T(8,128)(2,1)} async-done(((bf16[16,2,256,128]{3,2,1,0:T(8,128)(2,1)}), bf16[16,2,256,128]{3,2,1,0:T(8,128)(2,1)}, u32[]{:S(2)}, u32[]{:S(2)}) %all-to-all-start) | async-done | bytes 2097184 | tf_op jit(solution)/shard_map/all_to_all | solution.py:57
  118.7 1.7 copy.96
  120.4 0.0 copy-done.6
  120.4 1.9 convert_bitcast_fusion
  122.3 1.2 copy.46
  123.5 1.3 fusion.17
  124.8 1.1 subtract_convert_fusion.2
  125.9 3.4 %slice_bitcast_fusion.3 = (f32[65,64,128]{2,1,0:T(8,128)}, f32[65,64,128]{2,1,0:T(8,128)}, f32[65,64,128]{2,1,0:T(8,128)}, f32[65,64,128]{2,1,0:T(8,128)}) fusion(f32[65,128,2,128]{3,1,2,0:T(8,128)S(1)} %fusion.17), kind=kLoop, calls=%fused_computation.16 | loop fusion | bytes 17039360 | tf_op jit(solution)/shard_map/squeeze | solution.py:207
  129.4 0.0 copy-start.5
  129.4 0.7 fusion.25
  130.1 0.0 copy-done.5
  130.1 1.5 fusion.23
  131.6 1.4 copy.52
  133.1 1.3 fusion.22
  134.4 11.3 %all-to-all-start.1 = ((bf16[16,1,256,128]{3,2,1,0:T(8,128)(2,1)}), bf16[16,1,256,128]{3,2,1,0:T(8,128)(2,1)}, u32[]{:S(2)}, u32[]{:S(2)}) async-start(bf16[16,1,256,128]{3,2,1,0:T(8,128)(2,1)} %fusion.22), calls=%async_computation.1 | async-start | bytes 2097152 | tf_op jit(solution)/shard_map/all_to_all | solution.py:57
  145.6 6.4 %add_convert_fusion.1 = (bf16[65,64,128]{2,1,0:T(8,128)(2,1)S(1)}, bf16[65,64,128]{2,1,0:T(8,128)(2,1)S(1)}, bf16[65,64,128]{2,1,0:T(8,128)(2,1)S(1)}, bf16[65,64,128]{2,1,0:T(8,128)(2,1)S(1)}) fusion(f32[65,64,128]{2,1,0:T(8,128)} %get-tuple-element.17, f32[65,64,128]{2,1,0:T(8,128)} %get-tuple-element.16, f32[65,128,1,128]{3,1,0,2:T(8,128)} %convolution_bitcast_fusion, ...), kind=kLoop, calls=%fused_computation.31 | loop fusion | flops 8519680 | bytes 17039360 | tf_op jit(solution)/shard_map/convert.13
  152.1 0.8 maximum_bitcast_fusion
  152.9 0.0 copy-start.4
  152.9 1.5 fusion.5
  154.4 0.0 copy-done.4
  154.5 4.6 %fusion.4 = f32[2,64,64,128]{3,1,0,2:T(8,128)S(1)} fusion(bf16[2,65,64,1,1]{1,2,0,4,3:T(8,128)(2,1)S(1)} %copy-done.4, bf16[65,2,64,2,128]{4,2,1,3,0:T(8,128)(2,1)S(1)} %bitcast.148), kind=kOutput, calls=%fused_computation.7 | convolution fusion | flops 273678336 | bytes 8470784 | tf_op jit(solution)/shard_map/pfa,fpbsc->sabc/dot_general | solution.py:52
  159.0 0.2 slice.94
  159.3 0.1 slice.50
  159.4 0.7 copy.59
  160.1 1.2 copy.58
  161.3 0.3 fusion.20
  161.6 1.5 maximum_bitcast_fusion.2
  163.1 5.5 %all-to-all-done.1.refs_2_ = bf16[16,1,256,128]{3,2,1,0:T(8,128)(2,1)} async-done(((bf16[16,1,256,128]{3,2,1,0:T(8,128)(2,1)}), bf16[16,1,256,128]{3,2,1,0:T(8,128)(2,1)}, u32[]{:S(2)}, u32[]{:S(2)}) %all-to-all-start.1) | async-done | bytes 1048608 | tf_op jit(solution)/shard_map/all_to_all | solution.py:57
  168.6 6.8 %all-to-all-start.3 = ((bf16[16,2,256,128]{3,2,1,0:T(8,128)(2,1)}), bf16[16,2,256,128]{3,2,1,0:T(8,128)(2,1)S(1)}, u32[]{:S(2)}, u32[]{:S(2)}) async-start(bf16[16,2,256,128]{3,2,1,0:T(8,128)(2,1)} %maximum_bitcast_fusion.2), calls=%async_computation.3 | async-start | bytes 4194304 | tf_op jit(solution)/shard_map/all_to_all | solution.py:57
  175.4 4.3 %shard_map.138 = (bf16[256,2048]{1,0:T(8,128)(2,1)}, bf16[256,2048]{1,0:T(8,128)(2,1)}) custom-call(f32[256,2048]{1,0:T(8,128)} %fusion.32.refs_0_, bf16[256,2048]{1,0:T(8,128)(2,1)} %refs_1_.6, bf16[16,1,256,128]{3,2,1,0:T(8,128)(2,1)} %all-to-all-done.1.refs_2_), custom_call_target="tpu_custom_call" | custom-call | flops 4194304 | bytes 6291456 | tf_op jit(solution)/shard_map/pallas_call | solution.py:108
  179.6 8.4 %fusion.33 = f32[256,4096]{1,0:T(8,128)S(1)} fusion(bf16[256,2048]{1,0:T(8,128)(2,1)} %get-tuple-element.14, bf16[2048,4096]{1,0:T(8,128)(2,1)} %param.15), kind=kOutput, calls=%fused_computation.55 | convolution fusion | flops 4294967296 | bytes 22020096 | tf_op jit(solution)/shard_map/dot_general | solution.py:226
  188.1 0.0 copy-start.2
  188.1 1.9 copy-done.2
  190.0 1.1 dynamic-slice_convert_fusion
  191.1 1.5 collective-permute-start.1
  192.6 24.2 %collective-permute-done.1 = bf16[256,2048]{1,0:T(8,128)(2,1)S(1)} collective-permute-done((bf16[256,2048]{1,0:T(8,128)(2,1)}, bf16[256,2048]{1,0:T(8,128)(2,1)S(1)}, u32[]{:S(2)}, u32[]{:S(2)}) %collective-permute-start.1) | collective-permute-done | bytes 1048608 | tf_op jit(solution)/shard_map/ppermute | solution.py:146
  216.8 2.9 %add_convert_fusion.3 = bf16[256,2048]{1,0:T(8,128)(2,1)} fusion(bf16[256,2048]{1,0:T(8,128)(2,1)S(1)} %collective-permute-done.1, f32[256,4096]{1,0:T(8,128)} %copy-done.2, s32[]{:T(128)S(6)} %select_n.31), kind=kLoop, calls=%fused_computation.45 | loop fusion | flops 1572864 | bytes 4194308 | tf_op jit(solution)/shard_map/convert_element_type | solution.py:227
  219.6 0.0 all-to-all-done.3.refs_2_
  219.6 0.0 copy-start.1
  219.6 1.3 copy-done.1
  221.0 4.5 %shard_map.140 = (bf16[256,2048]{1,0:T(8,128)(2,1)}, bf16[256,2048]{1,0:T(8,128)(2,1)}, bf16[256,2048]{1,0:T(8,128)(2,1)}) custom-call(bf16[256,2048]{1,0:T(8,128)(2,1)} %refs_0_.3, bf16[256,2048]{1,0:T(8,128)(2,1)} %refs_1_.7, bf16[16,2,256,128]{3,2,1,0:T(8,128)(2,1)} %copy-done.1), custom_call_target="tpu_custom_call" | custom-call | flops 4194304 | bytes 7340032 | tf_op jit(solution)/shard_map/pallas_call | solution.py:108
Async XLA Ops:
  0.6 3.3 %copy-start.3 = (bf16[256,2048]{1,0:T(8,128)(2,1)S(1)}, bf16[256,2048]{1,0:T(8,128)(2,1)}, u32[]{:S(2)}) copy-start(bf16[256,2048]{1,0:T(8,128)(2,1)} %param.16) | copy-start | bytes 3145732
  0.6 26.5 %collective-permute-start = (bf16[256,2048]{1,0:T(8,128)(2,1)}, bf16[256,2048]{1,0:T(8,128)(2,1)}, u32[]{:S(2)}, u32[]{:S(2)}) collective-permute-start(bf16[256,2048]{1,0:T(8,128)(2,1)} %param.16), channel_id=1, source_target_pairs={{0,1},{1,0},{2,3},{3,2},{4,5},{5,4},{6,7},{7,6},{8,9},{9,8},{10,11... | collective-permute-start | bytes 3145736 | tf_op jit(solution)/shard_map/ppermute | solution.py:146
  41.8 29.0 %all-to-all-start.2 = ((bf16[16,1,256,128]{3,2,1,0:T(8,128)(2,1)}), bf16[16,1,256,128]{3,2,1,0:T(8,128)(2,1)S(1)}, u32[]{:S(2)}, u32[]{:S(2)}) async-start(bf16[16,1,256,128]{3,2,1,0:T(8,128)(2,1)} %shard_map.139), calls=%async_computation.2 | async-start | bytes 2097152 | tf_op jit(solution)/shard_map/all_to_all | solution.py:57
  52.0 26.5 %copy-start.7 = (bf16[2,65,64,1]{1,2,0,3:T(8,128)(2,1)S(1)}, bf16[2,65,64,1]{1,2,0,3:T(8,128)(2,1)}, u32[]{:S(2)}) copy-start(bf16[2,65,64,1]{1,2,0,3:T(8,128)(2,1)} %constant.55) | copy-start | bytes 49924
  70.8 47.9 %all-to-all-start = ((bf16[16,2,256,128]{3,2,1,0:T(8,128)(2,1)}), bf16[16,2,256,128]{3,2,1,0:T(8,128)(2,1)}, u32[]{:S(2)}, u32[]{:S(2)}) async-start(bf16[16,2,256,128]{3,2,1,0:T(8,128)(2,1)} %shard_map.137), calls=%async_computation | async-start | bytes 4194304 | tf_op jit(solution)/shard_map/all_to_all | solution.py:57
  79.6 1.6 copy-start
  84.1 36.3 %copy-start.6 = (bf16[2,65,64,1,1]{1,2,0,4,3:T(8,128)(2,1)S(1)}, bf16[2,65,64,1,1]{1,2,0,4,3:T(8,128)(2,1)}, u32[]{:S(2)}) copy-start(bf16[2,65,64,1,1]{1,2,0,4,3:T(8,128)(2,1)} %constant.53) | copy-start | bytes 49924
  129.4 0.8 copy-start.5
  134.4 34.2 %all-to-all-start.1 = ((bf16[16,1,256,128]{3,2,1,0:T(8,128)(2,1)}), bf16[16,1,256,128]{3,2,1,0:T(8,128)(2,1)}, u32[]{:S(2)}, u32[]{:S(2)}) async-start(bf16[16,1,256,128]{3,2,1,0:T(8,128)(2,1)} %fusion.22), calls=%async_computation.1 | async-start | bytes 2097152 | tf_op jit(solution)/shard_map/all_to_all | solution.py:57
  152.9 1.5 copy-start.4
  168.6 51.1 %all-to-all-start.3 = ((bf16[16,2,256,128]{3,2,1,0:T(8,128)(2,1)}), bf16[16,2,256,128]{3,2,1,0:T(8,128)(2,1)S(1)}, u32[]{:S(2)}, u32[]{:S(2)}) async-start(bf16[16,2,256,128]{3,2,1,0:T(8,128)(2,1)} %maximum_bitcast_fusion.2), calls=%async_computation.3 | async-start | bytes 4194304 | tf_op jit(solution)/shard_map/all_to_all | solution.py:57
  188.1 1.9 copy-start.2
  191.1 25.7 %collective-permute-start.1 = (bf16[256,2048]{1,0:T(8,128)(2,1)}, bf16[256,2048]{1,0:T(8,128)(2,1)S(1)}, u32[]{:S(2)}, u32[]{:S(2)}) collective-permute-start(bf16[256,2048]{1,0:T(8,128)(2,1)} %dynamic-slice_convert_fusion), channel_id=1, source_target_pairs={{0,1},{1,0},{2,3},{3,2},{4,5},{5,4},{6,7},{7,6},{8,9},{9,8},{10,11... | collective-permute-start | bytes 3145736 | tf_op jit(solution)/shard_map/ppermute | solution.py:146
  219.6 1.3 copy-start.1

commit v3 on v2

--- a/solution.py
+++ b/solution.py
@@ -26,14 +26,22 @@
 
 def inner_table(first, second):
     period = first * second
-    f1 = np.arange(first // 2 + 1)[:, None, None]
-    f2 = np.arange(second)[None, :, None]
-    b = np.arange(second)[None, None, :]
-    angles = (b * (f1 + first * f2) % period) * (2.0 * math.pi / period)
-    cosine, sine = np.cos(angles), np.sin(angles)
-    top = np.concatenate([cosine, sine], axis=2)
-    bottom = np.concatenate([-sine, cosine], axis=2)
-    return np.concatenate([top, bottom], axis=1)
+    f1 = np.arange(first // 2 + 1)[:, None]
+    f2 = np.arange(second)[:, None]
+    b = np.arange(second)[None, :]
+    slow = (b * f1 % period) * (2.0 * math.pi / period)
+    fast = (b * f2 % second) * (2.0 * math.pi / second)
+    cosine, sine = np.cos(fast), np.sin(fast)
+    small = (
+        np.tile(np.cos(slow), 2),
+        np.tile(np.sin(slow), 2),
+        np.block([[cosine, sine], [-sine, cosine]]),
+        np.block([[-sine, cosine], [-cosine, -sine]]),
+    )
+    small = lax.optimization_barrier(tuple(jnp.asarray(v, f32) for v in small))
+    by_cosine, by_sine = small[0][:, None], small[1][:, None]
+    table = (by_cosine * small[2][None] + by_sine * small[3][None]).astype(bf16)
+    return lax.optimization_barrier(table)
 
 
 def forward(signal, outer, inner):
@@ -146,26 +154,37 @@
     return lax.ppermute(value, "ch", [(i, (i + shift) % size) for i in range(size)])
 
 
-def gather_columns(value):
+def mixed_gradient(cotangent, out_weight):
     size, me = lax.axis_size("ch"), lax.axis_index("ch")
-    rows, width = value.shape
-    full = jnp.zeros((rows, size * width), value.dtype)
+    width = cotangent.shape[1]
+    total = None
     for shift in range(size):
-        part = shifted(value, shift) if shift else value
+        part = shifted(cotangent, shift) if shift else cotangent
         owner = (me - shift + size) % size
-        full = lax.dynamic_update_slice(full, part, (0, owner * width))
-    return full
-
-
-def scatter_columns(value):
+        weight = lax.dynamic_slice_in_dim(out_weight, owner * width, width, 1)
+        term = lax.dot_general(
+            part, weight, (((1,), (1,)), ((), ())), preferred_element_type=f32
+        )
+        total = term if total is None else total + term
+    return total
+
+
+def projection(gated, out_weight):
     size, me = lax.axis_size("ch"), lax.axis_index("ch")
-    rows, width = value.shape[0], value.shape[1] // size
-    total = lax.dynamic_slice(value, (0, me * width), (rows, width))
+    width = out_weight.shape[1] // size
+
+    def columns(target):
+        weight = lax.dynamic_slice_in_dim(out_weight, target * width, width, 1)
+        return jnp.dot(gated, weight, preferred_element_type=f32)
+
+    arrived = []
     for shift in range(1, size):
-        target = (me + shift) % size
-        part = lax.dynamic_slice(value, (0, target * width), (rows, width)).astype(bf16)
-        total = total + shifted(part, shift).astype(f32)
-    return total
+        part = columns((me + shift) % size).astype(bf16)
+        arrived.append(shifted(part, shift))
+    total = lax.optimization_barrier(columns(me))
+    for part in arrived:
+        total = total + part.astype(f32)
+    return total.astype(bf16)
 
 
 def on_device(queries, key_in, value_in, filter_raw, skip_gain, out_weight, cotangent):
@@ -179,7 +198,7 @@
     weight[0] = weight[-1] = 1.0
     outer = jnp.asarray(table, bf16)
     outer_back = jnp.asarray(table * weight, bf16)
-    inner = lax.optimization_barrier(jnp.asarray(inner_table(first, second), bf16))
+    inner = inner_table(first, second)
     factor = 1.0 / (math.sqrt(length) * 2.0 * length)
     skip_part = lax.dynamic_slice(skip_gain, (lax.axis_index("seq") * group,), (group,))
 
@@ -194,10 +213,7 @@
     got = exchange(sent)
     held = held_form(got)
 
-    gathered = gather_columns(cotangent)
-    grad_mixed = lax.dot_general(
-        gathered, out_weight, (((1,), (1,)), ((), ())), preferred_element_type=f32
-    )
+    grad_mixed = mixed_gradient(cotangent, out_weight)
     (sent,) = grouped(pack_gradient, [grad_mixed, queries], [], [], [(1, bf16)])
     got = exchange(sent)
     held_grad = held_form(got)
@@ -223,8 +239,7 @@
     gated_output, grad_query = grouped(
         unpack_convolved, [grad_mixed, queries], [convolved], [bf16, bf16], []
     )
-    partial_terms = jnp.dot(gated_output, out_weight, preferred_element_type=f32)
-    projected = scatter_columns(partial_terms).astype(bf16)
+    projected = projection(gated_output, out_weight)
     grad_key, grad_value, grad_filter = grouped(
         unpack_gradients, [key_in, value_in], [two], [bf16, bf16, bf16], []
     )

time: 229 us -> 225 us (0.983)
  the two profiles are of different devices: /device:TPU:0 before, /device:TPU:11 now
where the time goes in v3:
time: 225 us; the launch traced here: 224 us
  waiting for transfers between devices  112 us (50%)
  matrix products  41.6 us (18%)
  starting transfers between devices  24.4 us (11%)
  Pallas kernels  16.7 us (7%)
  other arithmetic  15.4 us (7%)
  local copies, waits for them, and re-layouts  12.7 us (6%)
    all_to_all x4, waiting for transfers between devices, exchange(): return lax.all_to_all(value, 'seq', split_axis=0, concat_axis=0, tiled=True)  78 us
    ppermute x2, waiting for transfers between devices, shifted(): lax.ppermute(value, 'ch', [(i, (i + shift) % size) for i in range(size)])  34.3 us
    all_to_all x4, starting transfers between devices, exchange(): return lax.all_to_all(value, 'seq', split_axis=0, concat_axis=0, tiled=True)  21.8 us
    pallas_call x4, Pallas kernels, grouped(): pl.pallas_call(kernel, grid=(groups // step,), in_specs=[flat_spec] * len...  16.7 us
    dot_general x2, matrix products, mixed_gradient(): lax.dot_general(part, weight, (((1,), (1,)), ((), ())), preferred_element...  13.1 us
    dot_general x2, matrix products, columns(): return jnp.dot(gated, weight, preferred_element_type=f32)  13.1 us
    another operation x3, other arithmetic  7.8 us
    dot_general x2, matrix products, inverse(): out = jnp.einsum('pfa,fpbsc->sabc', outer, mid, preferred_element_type=f32)  6.09 us
  transfers between devices with their start and end apart: 6, of which 6 were waited for; matrix products, arithmetic and copies ran while one was open for 20% of the time, Pallas kernels for 4%

profile of v3, /device:TPU:11, one launch (start us, length us, event | category | flops | bytes accessed | tf_op | source)
XLA Modules:
  0.0 224.0 jit_solution(7328506473150580540)
XLA Ops:
  0.6 1.3 collective-permute-start
  1.9 6.0 %fusion.2 = f32[2048,256]{0,1:T(8,128)S(1)} fusion(bf16[256,2048]{1,0:T(8,128)(2,1)} %param.19, bf16[2048,4096]{1,0:T(8,128)(2,1)} %param.18, s32[]{:T(128)S(6)} %select_n.27), kind=kOutput, calls=%fused_computation.2 | convolution fusion | flops 2147483648 | bytes 11534340 | tf_op jit(solution)/shard_map/dot_general | solution.py:165
  7.9 17.0 %collective-permute-done = bf16[256,2048]{1,0:T(8,128)(2,1)S(1)} collective-permute-done((bf16[256,2048]{1,0:T(8,128)(2,1)}, bf16[256,2048]{1,0:T(8,128)(2,1)S(1)}, u32[]{:S(2)}, u32[]{:S(2)}) %collective-permute-start) | collective-permute-done | bytes 1048608 | tf_op jit(solution)/shard_map/ppermute | solution.py:154
  25.0 7.1 %fusion.19.refs_0_ = f32[256,2048]{1,0:T(8,128)} fusion(f32[2048,256]{0,1:T(8,128)S(1)} %fusion.2, bf16[256,2048]{1,0:T(8,128)(2,1)S(1)} %collective-permute-done, bf16[2048,4096]{1,0:T(8,128)(2,1)} %param.18, s32[]{:T(128)S(6)} %select_n.29), kind=kOutput, calls=%fused_computation.19 | convolution fusion | flops 2148007936 | bytes 13631492 | tf_op jit(solution)/shard_map/dot_general | solution.py:165
  32.1 3.8 %shard_map.166 = bf16[16,1,256,128]{3,2,1,0:T(8,128)(2,1)} custom-call(f32[256,2048]{1,0:T(8,128)} %fusion.19.refs_0_, bf16[256,2048]{1,0:T(8,128)(2,1)} %refs_1_.6), custom_call_target="tpu_custom_call" | custom-call | flops 4194304 | bytes 4194304 | tf_op jit(solution)/shard_map/pallas_call | solution.py:116
  35.9 7.4 %all-to-all-start.2 = ((bf16[16,1,256,128]{3,2,1,0:T(8,128)(2,1)}), bf16[16,1,256,128]{3,2,1,0:T(8,128)(2,1)S(1)}, u32[]{:S(2)}, u32[]{:S(2)}) async-start(bf16[16,1,256,128]{3,2,1,0:T(8,128)(2,1)} %shard_map.166), calls=%async_computation.2 | async-start | bytes 2097152 | tf_op jit(solution)/shard_map/all_to_all | solution.py:65
  43.2 4.2 %shard_map.164 = bf16[16,2,256,128]{3,2,1,0:T(8,128)(2,1)} custom-call(bf16[256,2048]{1,0:T(8,128)(2,1)} %refs_0_.3, bf16[256,2048]{1,0:T(8,128)(2,1)} %refs_1_.7, bf16[256,2048]{1,0:T(8,128)(2,1)} %refs_2_.1), custom_call_target="tpu_custom_call" | custom-call | flops 4194304 | bytes 5242880 | tf_op jit(solution)/shard_map/pallas_call | solution.py:116
  47.4 0.0 copy-start.1
  47.4 0.0 copy-start.2
  47.4 0.0 copy-start.3
  47.4 0.0 copy-start.4
  47.4 20.7 %all-to-all-done.2 = bf16[16,1,256,128]{3,2,1,0:T(8,128)(2,1)S(1)} async-done(((bf16[16,1,256,128]{3,2,1,0:T(8,128)(2,1)}), bf16[16,1,256,128]{3,2,1,0:T(8,128)(2,1)S(1)}, u32[]{:S(2)}, u32[]{:S(2)}) %all-to-all-start.2) | async-done | bytes 1048608 | tf_op jit(solution)/shard_map/all_to_all | solution.py:65
  68.1 4.8 %all-to-all-start = ((bf16[16,2,256,128]{3,2,1,0:T(8,128)(2,1)}), bf16[16,2,256,128]{3,2,1,0:T(8,128)(2,1)}, u32[]{:S(2)}, u32[]{:S(2)}) async-start(bf16[16,2,256,128]{3,2,1,0:T(8,128)(2,1)} %shard_map.164), calls=%async_computation | async-start | bytes 4194304 | tf_op jit(solution)/shard_map/all_to_all | solution.py:65
  72.9 0.0 copy-start.8
  72.9 0.0 copy-done.1
  72.9 0.0 copy-done.2
  73.0 0.0 copy-done.3
  73.0 0.0 copy-done.4
  73.0 2.7 %add_convert_fusion = bf16[65,128,128]{1,2,0:T(8,128)(2,1)S(1)} fusion(f32[128,128]{0,1:T(8,128)S(1)} %copy-done.2, f32[65,128]{1,0:T(8,128)S(1)} %copy-done.4, f32[128,128]{0,1:T(8,128)S(1)} %copy-done.1, f32[65,128]{1,0:T(8,128)S(1)} %copy-done.3), kind=kLoop, calls=%fused_computation.14 | loop fusion | flops 4259840 | bytes 2327552 | tf_op jit(solution)/shard_map/convert_element_type | solution.py:43
  75.7 0.8 dynamic_slice.15
  76.4 0.0 copy-done.8
  76.5 1.0 convert_bitcast_fusion.1
  77.5 0.6 copy.63
  78.0 2.9 %convolution_bitcast_fusion = f32[65,128,1,128]{3,1,0,2:T(8,128)} fusion(bf16[65,128,128]{1,2,0:T(8,128)(2,1)S(1)} %add_convert_fusion, bf16[65,128,128]{2,1,0:T(8,128)(2,1)S(1)} %bitcast.144), kind=kOutput, calls=%fused_computation.24 | convolution fusion | flops 272629760 | bytes 8519680 | tf_op jit(solution)/shard_map/fxy,fysc->fxsc/dot_general | solution.py:53
  80.9 0.0 copy-start.7
  80.9 39.5 %all-to-all-done = bf16[16,2,256,128]{3,2,1,0:T(8,128)(2,1)} async-done(((bf16[16,2,256,128]{3,2,1,0:T(8,128)(2,1)}), bf16[16,2,256,128]{3,2,1,0:T(8,128)(2,1)}, u32[]{:S(2)}, u32[]{:S(2)}) %all-to-all-start) | async-done | bytes 2097184 | tf_op jit(solution)/shard_map/all_to_all | solution.py:65
  120.4 1.7 copy.107
  122.2 0.0 copy-done.7
  122.2 1.9 convert_bitcast_fusion
  124.1 1.2 copy.55
  125.3 1.3 fusion.34
  126.6 1.1 subtract_convert_fusion.2
  127.7 3.4 %slice_bitcast_fusion.3 = (f32[65,64,128]{2,1,0:T(8,128)}, f32[65,64,128]{2,1,0:T(8,128)}, f32[65,64,128]{2,1,0:T(8,128)}, f32[65,64,128]{2,1,0:T(8,128)}) fusion(f32[65,128,2,128]{3,1,2,0:T(8,128)S(1)} %fusion.34), kind=kLoop, calls=%fused_computation.28 | loop fusion | bytes 17039360 | tf_op jit(solution)/shard_map/squeeze | solution.py:223
  131.2 0.0 copy-start.6
  131.2 0.7 fusion.42
  131.9 0.0 copy-done.6
  131.9 1.5 fusion.40
  133.4 1.4 copy.61
  134.9 1.3 fusion.39
  136.1 4.8 %all-to-all-start.1 = ((bf16[16,1,256,128]{3,2,1,0:T(8,128)(2,1)}), bf16[16,1,256,128]{3,2,1,0:T(8,128)(2,1)}, u32[]{:S(2)}, u32[]{:S(2)}) async-start(bf16[16,1,256,128]{3,2,1,0:T(8,128)(2,1)} %fusion.39), calls=%async_computation.1 | async-start | bytes 2097152 | tf_op jit(solution)/shard_map/all_to_all | solution.py:65
  140.9 6.4 %add_convert_fusion.2 = (bf16[65,64,128]{2,1,0:T(8,128)(2,1)S(1)}, bf16[65,64,128]{2,1,0:T(8,128)(2,1)S(1)}, bf16[65,64,128]{2,1,0:T(8,128)(2,1)S(1)}, bf16[65,64,128]{2,1,0:T(8,128)(2,1)S(1)}) fusion(f32[65,64,128]{2,1,0:T(8,128)} %get-tuple-element.25, f32[65,64,128]{2,1,0:T(8,128)} %get-tuple-element.24, f32[65,128,1,128]{3,1,0,2:T(8,128)} %convolution_bitcast_fusion, ...), kind=kLoop, calls=%fused_computation.43 | loop fusion | flops 8519680 | bytes 17039360 | tf_op jit(solution)/shard_map/convert.13
  147.4 0.8 maximum_bitcast_fusion
  148.2 0.0 copy-start.5
  148.3 1.5 fusion.13
  149.8 0.0 copy-done.5
  149.8 4.6 %fusion.12 = f32[2,64,64,128]{3,1,0,2:T(8,128)S(1)} fusion(bf16[2,65,64,1,1]{1,2,0,4,3:T(8,128)(2,1)S(1)} %copy-done.5, bf16[65,2,64,2,128]{4,2,1,3,0:T(8,128)(2,1)S(1)} %bitcast.146), kind=kOutput, calls=%fused_computation.16 | convolution fusion | flops 273678336 | bytes 8470784 | tf_op jit(solution)/shard_map/pfa,fpbsc->sabc/dot_general | solution.py:60
  154.4 0.2 slice.94
  154.6 0.1 slice.50
  154.7 0.7 copy.68
  155.4 1.2 copy.67
  156.6 0.3 fusion.37
  156.9 1.5 maximum_bitcast_fusion.2
  158.4 7.5 %all-to-all-done.1.refs_2_ = bf16[16,1,256,128]{3,2,1,0:T(8,128)(2,1)} async-done(((bf16[16,1,256,128]{3,2,1,0:T(8,128)(2,1)}), bf16[16,1,256,128]{3,2,1,0:T(8,128)(2,1)}, u32[]{:S(2)}, u32[]{:S(2)}) %all-to-all-start.1) | async-done | bytes 1048608 | tf_op jit(solution)/shard_map/all_to_all | solution.py:65
  165.9 4.8 %all-to-all-start.3 = ((bf16[16,2,256,128]{3,2,1,0:T(8,128)(2,1)}), bf16[16,2,256,128]{3,2,1,0:T(8,128)(2,1)S(1)}, u32[]{:S(2)}, u32[]{:S(2)}) async-start(bf16[16,2,256,128]{3,2,1,0:T(8,128)(2,1)} %maximum_bitcast_fusion.2), calls=%async_computation.3 | async-start | bytes 4194304 | tf_op jit(solution)/shard_map/all_to_all | solution.py:65
  170.7 4.3 %shard_map.165 = (bf16[256,2048]{1,0:T(8,128)(2,1)}, bf16[256,2048]{1,0:T(8,128)(2,1)}) custom-call(f32[256,2048]{1,0:T(8,128)} %fusion.19.refs_0_, bf16[256,2048]{1,0:T(8,128)(2,1)} %refs_1_.6, bf16[16,1,256,128]{3,2,1,0:T(8,128)(2,1)} %all-to-all-done.1.refs_2_), custom_call_target="tpu_custom_call" | custom-call | flops 4194304 | bytes 6291456 | tf_op jit(solution)/shard_map/pallas_call | solution.py:116
  175.0 7.0 %fusion.22 = bf16[256,2048]{1,0:T(8,128)(2,1)} fusion(bf16[256,2048]{1,0:T(8,128)(2,1)} %get-tuple-element.22, bf16[2048,4096]{1,0:T(8,128)(2,1)} %param.18, s32[]{:T(128)S(6)} %select_n.29), kind=kOutput, calls=%fused_computation.20 | convolution fusion | flops 2148007936 | bytes 10485764 | tf_op jit(solution)/shard_map/dot_general | solution.py:178
  182.0 1.2 collective-permute-start.1
  183.2 6.0 %fusion = f32[256,2048]{1,0:T(8,128)S(1)} fusion(bf16[256,2048]{1,0:T(8,128)(2,1)} %get-tuple-element.22, bf16[2048,4096]{1,0:T(8,128)(2,1)} %param.18, s32[]{:T(128)S(6)} %select_n.31), kind=kOutput, calls=%fused_computation | convolution fusion | flops 2147483648 | bytes 11534340 | tf_op jit(solution)/shard_map/dot_general | solution.py:178
  189.3 17.3 %collective-permute-done.1 = bf16[256,2048]{1,0:T(8,128)(2,1)S(1)} collective-permute-done((bf16[256,2048]{1,0:T(8,128)(2,1)}, bf16[256,2048]{1,0:T(8,128)(2,1)S(1)}, u32[]{:S(2)}, u32[]{:S(2)}) %collective-permute-start.1) | collective-permute-done | bytes 1048608 | tf_op jit(solution)/shard_map/ppermute | solution.py:154
  206.5 1.3 add_convert_fusion.4
  207.8 10.3 %all-to-all-done.3.refs_2_ = bf16[16,2,256,128]{3,2,1,0:T(8,128)(2,1)S(1)} async-done(((bf16[16,2,256,128]{3,2,1,0:T(8,128)(2,1)}), bf16[16,2,256,128]{3,2,1,0:T(8,128)(2,1)S(1)}, u32[]{:S(2)}, u32[]{:S(2)}) %all-to-all-start.3) | async-done | bytes 2097184 | tf_op jit(solution)/shard_map/all_to_all | solution.py:65
  218.2 0.0 copy-start
  218.2 1.3 copy-done
  219.5 4.5 %shard_map.167 = (bf16[256,2048]{1,0:T(8,128)(2,1)}, bf16[256,2048]{1,0:T(8,128)(2,1)}, bf16[256,2048]{1,0:T(8,128)(2,1)}) custom-call(bf16[256,2048]{1,0:T(8,128)(2,1)} %refs_0_.3, bf16[256,2048]{1,0:T(8,128)(2,1)} %refs_1_.7, bf16[16,2,256,128]{3,2,1,0:T(8,128)(2,1)} %copy-done), custom_call_target="tpu_custom_call" | custom-call | flops 4194304 | bytes 7340032 | tf_op jit(solution)/shard_map/pallas_call | solution.py:116
Async XLA Ops:
  0.6 24.3 %collective-permute-start = (bf16[256,2048]{1,0:T(8,128)(2,1)}, bf16[256,2048]{1,0:T(8,128)(2,1)S(1)}, u32[]{:S(2)}, u32[]{:S(2)}) collective-permute-start(bf16[256,2048]{1,0:T(8,128)(2,1)} %param.19), channel_id=1, source_target_pairs={{0,1},{1,0},{2,3},{3,2},{4,5},{5,4},{6,7},{7,6},{8,9},{9,8},{10,11... | collective-permute-start | bytes 3145736 | tf_op jit(solution)/shard_map/ppermute | solution.py:154
  35.9 32.2 %all-to-all-start.2 = ((bf16[16,1,256,128]{3,2,1,0:T(8,128)(2,1)}), bf16[16,1,256,128]{3,2,1,0:T(8,128)(2,1)S(1)}, u32[]{:S(2)}, u32[]{:S(2)}) async-start(bf16[16,1,256,128]{3,2,1,0:T(8,128)(2,1)} %shard_map.166), calls=%async_computation.2 | async-start | bytes 2097152 | tf_op jit(solution)/shard_map/all_to_all | solution.py:65
  47.4 25.5 %copy-start.1 = (f32[128,128]{0,1:T(8,128)S(1)}, f32[128,128]{0,1:T(8,128)}, u32[]{:S(2)}) copy-start(f32[128,128]{0,1:T(8,128)} %constant.58.clone) | copy-start | bytes 196612
  47.4 25.6 %copy-start.2 = (f32[128,128]{0,1:T(8,128)S(1)}, f32[128,128]{0,1:T(8,128)}, u32[]{:S(2)}) copy-start(f32[128,128]{0,1:T(8,128)} %constant.59.clone) | copy-start | bytes 196612
  47.4 25.6 %copy-start.3 = (f32[65,128]{1,0:T(8,128)S(1)}, f32[65,128]{1,0:T(8,128)}, u32[]{:S(2)}) copy-start(f32[65,128]{1,0:T(8,128)} %constant.56.clone) | copy-start | bytes 99844
  47.4 25.6 %copy-start.4 = (f32[65,128]{1,0:T(8,128)S(1)}, f32[65,128]{1,0:T(8,128)}, u32[]{:S(2)}) copy-start(f32[65,128]{1,0:T(8,128)} %constant.57.clone) | copy-start | bytes 99844
  68.1 52.4 %all-to-all-start = ((bf16[16,2,256,128]{3,2,1,0:T(8,128)(2,1)}), bf16[16,2,256,128]{3,2,1,0:T(8,128)(2,1)}, u32[]{:S(2)}, u32[]{:S(2)}) async-start(bf16[16,2,256,128]{3,2,1,0:T(8,128)(2,1)} %shard_map.164), calls=%async_computation | async-start | bytes 4194304 | tf_op jit(solution)/shard_map/all_to_all | solution.py:65
  72.9 3.5 %copy-start.8 = (bf16[2,65,64,1]{1,2,0,3:T(8,128)(2,1)S(1)}, bf16[2,65,64,1]{1,2,0,3:T(8,128)(2,1)}, u32[]{:S(2)}) copy-start(bf16[2,65,64,1]{1,2,0,3:T(8,128)(2,1)} %constant.62) | copy-start | bytes 49924
  80.9 41.3 %copy-start.7 = (bf16[2,65,64,1,1]{1,2,0,4,3:T(8,128)(2,1)S(1)}, bf16[2,65,64,1,1]{1,2,0,4,3:T(8,128)(2,1)}, u32[]{:S(2)}) copy-start(bf16[2,65,64,1,1]{1,2,0,4,3:T(8,128)(2,1)} %constant.60) | copy-start | bytes 49924
  131.2 0.8 copy-start.6
  136.1 29.8 %all-to-all-start.1 = ((bf16[16,1,256,128]{3,2,1,0:T(8,128)(2,1)}), bf16[16,1,256,128]{3,2,1,0:T(8,128)(2,1)}, u32[]{:S(2)}, u32[]{:S(2)}) async-start(bf16[16,1,256,128]{3,2,1,0:T(8,128)(2,1)} %fusion.39), calls=%async_computation.1 | async-start | bytes 2097152 | tf_op jit(solution)/shard_map/all_to_all | solution.py:65
  148.2 1.5 copy-start.5
  165.9 52.2 %all-to-all-start.3 = ((bf16[16,2,256,128]{3,2,1,0:T(8,128)(2,1)}), bf16[16,2,256,128]{3,2,1,0:T(8,128)(2,1)S(1)}, u32[]{:S(2)}, u32[]{:S(2)}) async-start(bf16[16,2,256,128]{3,2,1,0:T(8,128)(2,1)} %maximum_bitcast_fusion.2), calls=%async_computation.3 | async-start | bytes 4194304 | tf_op jit(solution)/shard_map/all_to_all | solution.py:65
  182.0 24.5 %collective-permute-start.1 = (bf16[256,2048]{1,0:T(8,128)(2,1)}, bf16[256,2048]{1,0:T(8,128)(2,1)S(1)}, u32[]{:S(2)}, u32[]{:S(2)}) collective-permute-start(bf16[256,2048]{1,0:T(8,128)(2,1)} %fusion.22), channel_id=1, source_target_pairs={{0,1},{1,0},{2,3},{3,2},{4,5},{5,4},{6,7},{7,6},{8,9},{9,8},{10,11... | collective-permute-start | bytes 3145736 | tf_op jit(solution)/shard_map/ppermute | solution.py:154
  218.2 1.3 copy-start
